TPU v7x, 128 devices: a whole 4x4x4 slice. The times are simulated.
128 devices in a mesh: ctx: 16 (over z_lo, y, core), ch: 8 (over z_hi, x).
Axes of the slice: x: 4, y: 4, z: 4 (z_hi: 2, z_lo: 2; z = z_hi * 2 + z_lo), core: 2. Of those that a mesh axis runs over, the one named last changes fastest.
Arguments:
- q_vals: bfloat16 [8192, 4096], P('ch', 'ctx'), may hold values from -6 to 6
- k_vals: bfloat16 [8192, 4096], P('ch', 'ctx'), may hold values from -6 to 6
- v_vals: bfloat16 [8192, 4096], P('ch', 'ctx'), may hold values from -6 to 6
- grad_out: bfloat16 [8192, 4096], P('ch', 'ctx'), may hold values from -6 to 6
- exponents: int32 [3, 64, 32], P(None, 'ch', 'ctx'), may hold values from -2 to 1
- filter_taps: float32 [512, 1024], P('ch'), may hold values from -1 to 1
Outputs:
- grad_q: bfloat16 [8192, 4096], P('ch', 'ctx')
- grad_k: bfloat16 [8192, 4096], P('ch', 'ctx')
- grad_v: bfloat16 [8192, 4096], P('ch', 'ctx')
- grad_filter: float32 [512, 1024], P('ch', 'ctx')
- grad_amax: float32 [3, 32], P(None, 'ctx')
All inputs are finite; a program needn't handle non-finite values.
Results may differ from a plain program's by a relative error of at most 0.0061.
Values may be sent and summed in bfloat16 or wider, within the bound.
No kernel may reach another device: no remote copies, remote signals or barrier semaphores. Data moves between devices by JAX's collectives and lax.ppermute only.
A program may use at most 128 MiB of HBM per device.

v0:
```python
import functools

import jax
import jax.numpy as jnp
from jax import lax
from jax.experimental import pallas as pl
from jax.experimental.pallas import tpu as pltpu
from jax.sharding import PartitionSpec as P

EPS = 1e-06
TILE = 128


def power(exponent):
    return lax.shift_left(jnp.int32(1), exponent + 8).astype(jnp.float32) * (2.0 ** -8)


def mirror():
    shape = (TILE, TILE)
    rows = lax.broadcasted_iota(jnp.int32, shape, 0)
    lanes = lax.broadcasted_iota(jnp.int32, shape, 1)
    return (rows + lanes == TILE - 1).astype(jnp.float32).astype(jnp.bfloat16)


def mirrored(values, flip, terms):
    pieces = []
    rest = values
    for _ in range(terms):
        piece = rest.astype(jnp.bfloat16)
        pieces.append(piece)
        rest = rest - piece.astype(jnp.float32)
    return jnp.dot(
        jnp.concatenate(pieces, axis=1),
        jnp.concatenate([flip] * terms, axis=0),
        preferred_element_type=jnp.float32,
    )


def squares(ref, block):
    for n in range(ref.shape[0] // block):
        for p in range(PARTS):
            yield n, p, slice(n * block, (n + 1) * block), slice(p * TILE, (p + 1) * TILE)


PARTS = 2


def gate_kernel(e_ref, q_ref, k_ref, v_ref, g_ref, out_ref, *, block):
    first = pl.program_id(0) * (q_ref.shape[0] // block)
    flip = mirror()
    for n, p, at, lanes in squares(q_ref, block):
        b = first + n
        q_real = q_ref[at, lanes].astype(jnp.float32) * power(e_ref[0, b, p])
        k_real = k_ref[at, lanes].astype(jnp.float32) * power(e_ref[1, b, p])
        v_real = v_ref[at, lanes].astype(jnp.float32) * power(e_ref[2, b, p])
        out_ref[at, lanes] = (k_real * v_real).astype(jnp.bfloat16)
        gw = (q_real * g_ref[at, lanes].astype(jnp.float32)).astype(jnp.bfloat16)
        o = 2 * PARTS - 1 - p
        out_ref[at, o * TILE : (o + 1) * TILE] = jnp.dot(
            gw, flip, preferred_element_type=jnp.float32
        ).astype(jnp.bfloat16)


def conv_kernel(taps_ref, x_ref, y_ref, lag_ref, toe_ref, z_ref, u_ref, b_ref):
    blocks, width = x_ref.shape[:2]
    taps = taps_ref.shape[2]
    span = taps + TILE
    tiles = span // TILE
    lead = tiles - 1
    count = blocks * PARTS

    row = taps_ref[0].astype(jnp.bfloat16).astype(jnp.float32)
    row = jnp.concatenate([row, jnp.zeros((1, TILE), jnp.float32)], axis=1)
    row = jnp.broadcast_to(row, (8, span))
    low = pltpu.roll(row, 0, 1, stride=1, stride_axis=0)
    high = pltpu.roll(row, 8, 1, stride=1, stride_axis=0)
    base = jnp.concatenate([low, high], axis=0).astype(jnp.bfloat16)
    for a in range(0, TILE, 16):
        rolled = pltpu.roll(base, a, 1) if a else base
        for d in range(tiles):
            toe_ref[d * TILE + a : d * TILE + a + 16, :] = rolled[:, d * TILE : (d + 1) * TILE]

    def z_tile(t):
        t = t % count
        return x_ref[t // PARTS, :, (t % PARTS) * TILE : (t % PARTS + 1) * TILE]

    def back_tile(t):
        t = t % count
        o = PARTS + t % PARTS
        return x_ref[blocks - 1 - t // PARTS, :, o * TILE : (o + 1) * TILE]

    for n in range(count + lead):
        rows = slice(n * width, (n + 1) * width)
        z_ref[rows, :] = z_tile(n - lead)
        b_ref[rows, :] = back_tile(n - lead)
        u_ref[rows, :] = z_tile(count - 1 - n)

    def window(ref):
        return jnp.concatenate(
            [ref[(lead - d) * width : (lead - d + count) * width, :] for d in range(tiles)], axis=1
        )

    w = jnp.dot(window(z_ref), toe_ref[...], preferred_element_type=jnp.float32)
    for t in range(count):
        y_ref[t // PARTS, :, (t % PARTS) * TILE : (t % PARTS + 1) * TILE] = w[
            t * width : (t + 1) * width, :
        ].astype(jnp.bfloat16)
    gz = jnp.dot(window(b_ref), toe_ref[...], preferred_element_type=jnp.float32)
    for t in range(count):
        o = PARTS + t % PARTS
        y_ref[blocks - 1 - t // PARTS, :, o * TILE : (o + 1) * TILE] = gz[
            t * width : (t + 1) * width, :
        ].astype(jnp.bfloat16)

    cross = lax.dot_general(
        b_ref[lead * width : (lead + count) * width, :],
        window(u_ref),
        (((0,), (0,)), ((), ())),
        preferred_element_type=jnp.float32,
    )
    total = None
    for a in range(0, TILE, 8):
        turned = pltpu.roll(
            cross[a : a + 8, :], (a + span - TILE) % span, 1, stride=1, stride_axis=0
        )
        total = turned if total is None else total + turned
    diag = jnp.sum(total, axis=0, keepdims=True)
    pieces = taps // TILE
    stacked = jnp.concatenate([diag[:, n * TILE : (n + 1) * TILE] for n in range(pieces)], axis=0)
    stacked = mirrored(stacked, mirror(), 3)
    for n in range(pieces):
        o = pieces - 1 - n
        lag_ref[0, o : o + 1, :] = stacked[n : n + 1, :]


def gradients(e_ref, k_ref, v_ref, g_ref, y_ref, block):
    first = pl.program_id(0) * (k_ref.shape[0] // block)
    flip = mirror()
    for n, p, at, lanes in squares(k_ref, block):
        o = 2 * PARTS - 1 - p
        w = y_ref[at, lanes].astype(jnp.float32)
        gz = jnp.dot(
            y_ref[at, o * TILE : (o + 1) * TILE], flip, preferred_element_type=jnp.float32
        )
        v_real = v_ref[at, lanes].astype(jnp.float32) * power(e_ref[2, first + n, p])
        k_real = k_ref[at, lanes].astype(jnp.float32) * power(e_ref[1, first + n, p])
        g = g_ref[at, lanes].astype(jnp.float32)
        yield p, at, lanes, (g * w, gz * v_real, gz * k_real)


def peak_kernel(e_ref, k_ref, v_ref, g_ref, y_ref, peak_ref, *, block):
    @pl.when(pl.program_id(0) == 0)
    def _():
        peak_ref[...] = jnp.zeros(peak_ref.shape, jnp.float32)

    for p, at, lanes, products in gradients(e_ref, k_ref, v_ref, g_ref, y_ref, block):
        for i, product in enumerate(products):
            top = jnp.max(jnp.abs(product), axis=0, keepdims=True)
            spot = slice(p * 4 + i, p * 4 + i + 1)
            peak_ref[spot, :] = jnp.maximum(peak_ref[spot, :], top)

    @pl.when(pl.program_id(0) == pl.num_programs(0) - 1)
    def _():
        best = jnp.max(peak_ref[...], axis=1, keepdims=True)
        peak_ref[...] = jnp.broadcast_to(best, peak_ref.shape)


def scale_kernel(e_ref, k_ref, v_ref, g_ref, y_ref, *refs, block):
    peaks, (oq_ref, ok_ref, ov_ref, top_ref) = refs[:-4], refs[-4:]
    top = peaks[0][...]
    for ref in peaks[1:]:
        top = jnp.maximum(top, ref[...])
    top_ref[...] = top
    inverse = 1.0 / (top + EPS)
    for p, at, lanes, products in gradients(e_ref, k_ref, v_ref, g_ref, y_ref, block):
        for i, (product, ref) in enumerate(zip(products, (oq_ref, ok_ref, ov_ref))):
            ref[at, lanes] = (product * inverse[p * 4 + i : p * 4 + i + 1, :]).astype(jnp.bfloat16)


def shards(q_vals, k_vals, v_vals, grad_out, exponents, filter_taps):
    channels, rows = q_vals.shape
    groups, taps = filter_taps.shape
    block = channels // exponents.shape[1]
    width = channels // groups
    ctx = lax.axis_size("ctx")
    ch = lax.axis_size("ch")
    part = channels // ctx
    mine = groups // ctx
    span = taps + TILE
    tall = 2 * block
    steps = (channels // tall,)
    scalars = pl.BlockSpec(memory_space=pltpu.SMEM)
    tile = pl.BlockSpec((tall, rows), lambda b: (b, 0))
    double = pl.BlockSpec((tall, 2 * rows), lambda b: (b, 0))
    whole = pl.BlockSpec((8, TILE), lambda b: (0, 0))
    bf16 = jnp.bfloat16

    gated = pl.pallas_call(
        functools.partial(gate_kernel, block=block),
        grid=steps,
        in_specs=[scalars] + [tile] * 4,
        out_specs=double,
        out_shape=jax.ShapeDtypeStruct((channels, 2 * rows), bf16),
        name="gate",
    )(exponents, q_vals, k_vals, v_vals, grad_out)
    swapped = lax.all_to_all(gated, "ctx", split_axis=0, concat_axis=0, tiled=True)

    own_taps = lax.dynamic_slice_in_dim(filter_taps, lax.axis_index("ctx") * mine, mine, 0)
    stack = pltpu.VMEM(((ctx * PARTS + taps // TILE) * width, TILE), bf16)
    seq = pl.BlockSpec((ctx, width, 2 * rows), lambda b: (0, b, 0))
    y, lag = pl.pallas_call(
        conv_kernel,
        grid=(mine,),
        in_specs=[pl.BlockSpec((1, 1, taps), lambda b: (b, 0, 0)), seq],
        out_specs=[seq, pl.BlockSpec((1, taps // TILE, TILE), lambda b: (b, 0, 0))],
        out_shape=[
            jax.ShapeDtypeStruct((ctx, part, 2 * rows), bf16),
            jax.ShapeDtypeStruct((mine, taps // TILE, TILE), jnp.float32),
        ],
        scratch_shapes=[pltpu.VMEM((span, TILE), bf16), stack, stack, stack],
        name="conv",
    )(own_taps.reshape(mine, 1, taps), swapped.reshape(ctx, part, 2 * rows))

    y = lax.all_to_all(y.reshape(channels, 2 * rows), "ctx", split_axis=0, concat_axis=0, tiled=True)
    pieces = lag.reshape(mine, ctx, taps // ctx).transpose(1, 0, 2)
    pieces = lax.all_to_all(pieces, "ctx", split_axis=0, concat_axis=0, tiled=True)
    grad_filter = pieces.reshape(groups, taps // ctx)

    peak = pl.pallas_call(
        functools.partial(peak_kernel, block=block),
        grid=steps,
        in_specs=[scalars] + [tile] * 3 + [double],
        out_specs=whole,
        out_shape=jax.ShapeDtypeStruct((8, TILE), jnp.float32),
        name="peak",
    )(exponents, k_vals, v_vals, grad_out, y)
    peaks = [peak]
    for by in range(1, ch):
        peaks.append(lax.ppermute(peak, "ch", [(i, (i + by) % ch) for i in range(ch)]))

    oq, ok, ov, top = pl.pallas_call(
        functools.partial(scale_kernel, block=block),
        grid=steps,
        in_specs=[scalars] + [tile] * 3 + [double] + [whole] * ch,
        out_specs=[tile] * 3 + [whole],
        out_shape=[jax.ShapeDtypeStruct((channels, rows), bf16)] * 3
        + [jax.ShapeDtypeStruct((8, TILE), jnp.float32)],
        name="scale",
    )(exponents, k_vals, v_vals, grad_out, y, *peaks)
    block_peak = top[:, 0].reshape(PARTS, 4)[:, :3].T
    return oq, ok, ov, grad_filter, block_peak


def solution(mesh):
    in_specs = (
        P("ch", "ctx"),
        P("ch", "ctx"),
        P("ch", "ctx"),
        P("ch", "ctx"),
        P(None, "ch", "ctx"),
        P("ch", None),
    )
    out_specs = (P("ch", "ctx"), P("ch", "ctx"), P("ch", "ctx"), P("ch", "ctx"), P(None, "ctx"))
    return jax.shard_map(shards, mesh=mesh, in_specs=in_specs, out_specs=out_specs, check_vma=False)
```

profile of v0, /device:TPU:0, one launch (start us, length us, event | category | flops | bytes accessed | tf_op | source)
XLA Modules:
  0.0 90.1 jit_solution(10335388916201940560)
XLA Ops:
  0.6 0.0 copy-start
  0.6 1.4 %copy.21.e_ref = s32[3,8,2]{2,1,0:T(8,128)} copy(s32[3,8,2]{1,2,0:T(2,128)} %param.10) | data formatting | bytes 384 | tf_op args[4]
  2.1 4.1 %gate.1 = bf16[1024,512]{1,0:T(8,128)(2,1)} custom-call(s32[3,8,2]{2,1,0:T(8,128)} %copy.21.e_ref, bf16[1024,256]{1,0:T(8,128)(2,1)} %q_ref.1, bf16[1024,256]{1,0:T(8,128)(2,1)} %k_ref.5, bf16[1024,256]{1,0:T(8,128)(2,1)} %v_ref.5, bf16[1024,256]{1,0:T(8,128)(2,1)} %g_ref.5), custom_call_target="tpu_custom_call" | custom-call | tf_op jit(solution)/shard_map/gate/pallas_call | solution.py:198
  6.1 6.0 %all-to-all-start = ((bf16[16,64,512]{2,1,0:T(8,128)(2,1)}), bf16[16,64,512]{2,1,0:T(8,128)(2,1)S(1)}, u32[]{:S(2)}, u32[]{:S(2)}) async-start(bf16[16,64,512]{2,1,0:T(8,128)(2,1)} %bitcast.10), calls=%async_computation | async-start | bytes 2097152 | tf_op jit(solution)/shard_map/all_to_all | solution.py:206
  12.1 0.0 copy-done
  12.2 0.6 reshape.27.taps_ref
  12.8 15.8 %all-to-all-done.x_ref = bf16[16,64,512]{2,1,0:T(8,128)(2,1)S(1)} async-done(((bf16[16,64,512]{2,1,0:T(8,128)(2,1)}), bf16[16,64,512]{2,1,0:T(8,128)(2,1)S(1)}, u32[]{:S(2)}, u32[]{:S(2)}) %all-to-all-start) | async-done | bytes 1048608 | tf_op jit(solution)/shard_map/all_to_all | solution.py:206
  28.6 0.0 copy-start.2
  28.6 1.0 %copy-done.2 = bf16[16,64,512]{2,1,0:T(8,128)(2,1)} copy-done((bf16[16,64,512]{2,1,0:T(8,128)(2,1)}, bf16[16,64,512]{2,1,0:T(8,128)(2,1)S(1)}, u32[]{:S(2)}) %copy-start.2) | copy-done | bytes 1048600
  29.6 7.1 %conv.1 = (bf16[16,64,512]{2,1,0:T(8,128)(2,1)}, f32[4,8,128]{2,1,0:T(8,128)}) custom-call(f32[4,1,1024]{2,1,0:T(1,128)} %reshape.27.taps_ref, bf16[16,64,512]{2,1,0:T(8,128)(2,1)} %copy-done.2), custom_call_target="tpu_custom_call" | custom-call | tf_op jit(solution)/shard_map/conv/pallas_call | solution.py:211
  36.7 0.0 copy-start.3
  36.7 3.8 %all-to-all-start.1 = ((bf16[16,64,512]{2,1,0:T(8,128)(2,1)}), bf16[16,64,512]{2,1,0:T(8,128)(2,1)S(1)}, u32[]{:S(2)}, u32[]{:S(2)}) async-start(bf16[16,64,512]{2,1,0:T(8,128)(2,1)} %get-tuple-element.11), calls=%async_computation.1 | async-start | bytes 2097152 | tf_op jit(solution)/shard_map/all_to_all | solution.py:224
  40.5 0.0 copy-done.3
  40.5 0.1 reshape.28
  40.6 0.7 reshape.31
  41.3 15.6 %all-to-all-done.1 = bf16[16,64,512]{2,1,0:T(8,128)(2,1)S(1)} async-done(((bf16[16,64,512]{2,1,0:T(8,128)(2,1)}), bf16[16,64,512]{2,1,0:T(8,128)(2,1)S(1)}, u32[]{:S(2)}, u32[]{:S(2)}) %all-to-all-start.1) | async-done | bytes 1048608 | tf_op jit(solution)/shard_map/all_to_all | solution.py:224
  56.9 0.0 copy-start.1
  56.9 3.5 %all-to-all-start.2 = ((f32[16,1,256]{2,1,0:T(1,128)}), f32[16,1,256]{2,1,0:T(1,128)S(1)}, u32[]{:S(2)}, u32[]{:S(2)}) async-start(f32[16,1,256]{2,1,0:T(1,128)} %reshape.31), calls=%async_computation.2 | async-start | bytes 32768 | tf_op jit(solution)/shard_map/all_to_all | solution.py:226
  60.4 0.0 copy-done.1
  60.4 3.7 %peak.1.refs_0_ = f32[8,128]{1,0:T(8,128)} custom-call(s32[3,8,2]{2,1,0:T(8,128)} %copy.21.e_ref, bf16[1024,256]{1,0:T(8,128)(2,1)} %k_ref.5, bf16[1024,256]{1,0:T(8,128)(2,1)} %v_ref.5, bf16[1024,256]{1,0:T(8,128)(2,1)} %g_ref.5, bf16[1024,512]{1,0:T(8,128)(2,1)} %bitcast.8), custom_call_target="tpu_custom_call" | custom-call | tf_op jit(solution)/shard_map/peak/pallas_call | solution.py:229
  64.1 1.5 %collective-permute-start = (f32[8,128]{1,0:T(8,128)}, f32[8,128]{1,0:T(8,128)S(1)}, u32[]{:S(2)}, u32[]{:S(2)}) collective-permute-start(f32[8,128]{1,0:T(8,128)} %peak.1.refs_0_), channel_id=1, source_target_pairs={{0,1},{1,2},{2,3},{3,4},{4,5},{5,6},{6,7},{7,0},{8,9},{9,10},{10,1... | collective-permute-start | bytes 12296 | tf_op jit(solution)/shard_map/ppermute | solution.py:239
  65.6 2.7 %collective-permute-start.1 = (f32[8,128]{1,0:T(8,128)}, f32[8,128]{1,0:T(8,128)S(1)}, u32[]{:S(2)}, u32[]{:S(2)}) collective-permute-start(f32[8,128]{1,0:T(8,128)} %peak.1.refs_0_), channel_id=1, source_target_pairs={{0,2},{1,3},{2,4},{3,5},{4,6},{5,7},{6,0},{7,1},{8,10},{9,11},{10,... | collective-permute-start | bytes 12296 | tf_op jit(solution)/shard_map/ppermute | solution.py:239
  68.3 4.5 %collective-permute-start.2 = (f32[8,128]{1,0:T(8,128)}, f32[8,128]{1,0:T(8,128)S(1)}, u32[]{:S(2)}, u32[]{:S(2)}) collective-permute-start(f32[8,128]{1,0:T(8,128)} %peak.1.refs_0_), channel_id=1, source_target_pairs={{0,3},{1,4},{2,5},{3,6},{4,7},{5,0},{6,1},{7,2},{8,11},{9,12},{10,... | collective-permute-start | bytes 12296 | tf_op jit(solution)/shard_map/ppermute | solution.py:239
  72.8 0.0 collective-permute-start.3
  72.8 3.6 %collective-permute-start.4 = (f32[8,128]{1,0:T(8,128)}, f32[8,128]{1,0:T(8,128)S(1)}, u32[]{:S(2)}, u32[]{:S(2)}) collective-permute-start(f32[8,128]{1,0:T(8,128)} %peak.1.refs_0_), channel_id=1, source_target_pairs={{0,5},{1,6},{2,7},{3,0},{4,1},{5,2},{6,3},{7,4},{8,13},{9,14},{10,... | collective-permute-start | bytes 12296 | tf_op jit(solution)/shard_map/ppermute | solution.py:239
  76.3 0.0 collective-permute-done.refs_1_
  76.3 0.0 copy-start.4
  76.3 3.2 %collective-permute-start.5 = (f32[8,128]{1,0:T(8,128)}, f32[8,128]{1,0:T(8,128)S(1)}, u32[]{:S(2)}, u32[]{:S(2)}) collective-permute-start(f32[8,128]{1,0:T(8,128)} %peak.1.refs_0_), channel_id=1, source_target_pairs={{0,6},{1,7},{2,0},{3,1},{4,2},{5,3},{6,4},{7,5},{8,14},{9,15},{10,... | collective-permute-start | bytes 12296 | tf_op jit(solution)/shard_map/ppermute | solution.py:239
  79.5 0.0 collective-permute-done.1.refs_2_
  79.5 0.0 copy-start.5
  79.5 1.7 %collective-permute-start.6 = (f32[8,128]{1,0:T(8,128)}, f32[8,128]{1,0:T(8,128)S(1)}, u32[]{:S(2)}, u32[]{:S(2)}) collective-permute-start(f32[8,128]{1,0:T(8,128)} %peak.1.refs_0_), channel_id=1, source_target_pairs={{0,7},{1,0},{2,1},{3,2},{4,3},{5,4},{6,5},{7,6},{8,15},{9,8},{10,9... | collective-permute-start | bytes 12296 | tf_op jit(solution)/shard_map/ppermute | solution.py:239
  81.3 0.0 all-to-all-done.2
  81.3 0.5 broadcast.1
  81.8 0.7 reduce.2
  82.5 0.0 copy-done.4
  82.5 0.0 copy-done.5
  82.5 0.7 reshape.32
  83.2 0.0 collective-permute-done.2.refs_3_
  83.2 0.0 copy-start.6
  83.2 0.0 collective-permute-done.3.refs_4_
  83.2 0.0 copy-start.7
  83.2 0.0 collective-permute-done.4.refs_5_
  83.2 0.0 copy-start.8
  83.3 0.0 collective-permute-done.5.refs_6_
  83.3 0.0 copy-start.9
  83.3 0.1 collective-permute-done.6.refs_7_
  83.4 0.4 copy-done.6
  83.8 0.0 copy-done.7
  83.8 0.0 copy-done.8
  83.8 0.0 copy-done.9
  83.9 0.0 copy-start.10
  83.9 0.6 copy-done.10
  84.4 4.2 %scale.1 = (bf16[1024,256]{1,0:T(8,128)(2,1)}, bf16[1024,256]{1,0:T(8,128)(2,1)}, bf16[1024,256]{1,0:T(8,128)(2,1)}, f32[8,128]{1,0:T(8,128)}) custom-call(s32[3,8,2]{2,1,0:T(8,128)} %copy.21.e_ref, bf16[1024,256]{1,0:T(8,128)(2,1)} %k_ref.5, bf16[1024,256]{1,0:T(8,128)(2,1)} %v_ref.5, bf16[1024,256]{1,0:T(8,128)(2,1)} %g_ref.5, bf16[1024,512]{1,0:T(8,128)(2,1)} %bitcast.9, ...), custom_call_target="tpu_custom_call" | custom-call | tf_op jit(solution)/shard_map/scale/pallas_call | solution.py:241
  88.7 0.8 slice_reduce_fusion
  89.5 0.1 reshape_squeeze.3
  89.6 0.6 slice_bitcast_fusion
  (2 shorter events, 0.0 us)
Async XLA Ops:
  0.6 11.5 %copy-start = (f32[64,1024]{1,0:T(8,128)S(1)}, f32[64,1024]{1,0:T(8,128)}, u32[]{:S(2)}) copy-start(f32[64,1024]{1,0:T(8,128)} %param.11) | copy-start | bytes 786436
  6.1 22.5 %all-to-all-start = ((bf16[16,64,512]{2,1,0:T(8,128)(2,1)}), bf16[16,64,512]{2,1,0:T(8,128)(2,1)S(1)}, u32[]{:S(2)}, u32[]{:S(2)}) async-start(bf16[16,64,512]{2,1,0:T(8,128)(2,1)} %bitcast.10), calls=%async_computation | async-start | bytes 2097152 | tf_op jit(solution)/shard_map/all_to_all | solution.py:206
  28.6 1.0 %copy-start.2 = (bf16[16,64,512]{2,1,0:T(8,128)(2,1)}, bf16[16,64,512]{2,1,0:T(8,128)(2,1)S(1)}, u32[]{:S(2)}) copy-start(bf16[16,64,512]{2,1,0:T(8,128)(2,1)S(1)} %all-to-all-done.x_ref) | copy-start | bytes 3145732
  36.7 3.8 %copy-start.3 = (f32[4,8,128]{2,1,0:T(8,128)S(1)}, f32[4,8,128]{2,1,0:T(8,128)}, u32[]{:S(2)}) copy-start(f32[4,8,128]{2,1,0:T(8,128)} %get-tuple-element.15) | copy-start | bytes 49156
  36.7 20.2 %all-to-all-start.1 = ((bf16[16,64,512]{2,1,0:T(8,128)(2,1)}), bf16[16,64,512]{2,1,0:T(8,128)(2,1)S(1)}, u32[]{:S(2)}, u32[]{:S(2)}) async-start(bf16[16,64,512]{2,1,0:T(8,128)(2,1)} %get-tuple-element.11), calls=%async_computation.1 | async-start | bytes 2097152 | tf_op jit(solution)/shard_map/all_to_all | solution.py:224
  56.9 3.5 %copy-start.1 = (bf16[16,64,512]{2,1,0:T(8,128)(2,1)}, bf16[16,64,512]{2,1,0:T(8,128)(2,1)S(1)}, u32[]{:S(2)}) copy-start(bf16[16,64,512]{2,1,0:T(8,128)(2,1)S(1)} %all-to-all-done.1) | copy-start | bytes 3145732
  56.9 24.4 %all-to-all-start.2 = ((f32[16,1,256]{2,1,0:T(1,128)}), f32[16,1,256]{2,1,0:T(1,128)S(1)}, u32[]{:S(2)}, u32[]{:S(2)}) async-start(f32[16,1,256]{2,1,0:T(1,128)} %reshape.31), calls=%async_computation.2 | async-start | bytes 32768 | tf_op jit(solution)/shard_map/all_to_all | solution.py:226
  64.1 12.2 %collective-permute-start = (f32[8,128]{1,0:T(8,128)}, f32[8,128]{1,0:T(8,128)S(1)}, u32[]{:S(2)}, u32[]{:S(2)}) collective-permute-start(f32[8,128]{1,0:T(8,128)} %peak.1.refs_0_), channel_id=1, source_target_pairs={{0,1},{1,2},{2,3},{3,4},{4,5},{5,6},{6,7},{7,0},{8,9},{9,10},{10,1... | collective-permute-start | bytes 12296 | tf_op jit(solution)/shard_map/ppermute | solution.py:239
  65.6 14.0 %collective-permute-start.1 = (f32[8,128]{1,0:T(8,128)}, f32[8,128]{1,0:T(8,128)S(1)}, u32[]{:S(2)}, u32[]{:S(2)}) collective-permute-start(f32[8,128]{1,0:T(8,128)} %peak.1.refs_0_), channel_id=1, source_target_pairs={{0,2},{1,3},{2,4},{3,5},{4,6},{5,7},{6,0},{7,1},{8,10},{9,11},{10,... | collective-permute-start | bytes 12296 | tf_op jit(solution)/shard_map/ppermute | solution.py:239
  68.3 14.9 %collective-permute-start.2 = (f32[8,128]{1,0:T(8,128)}, f32[8,128]{1,0:T(8,128)S(1)}, u32[]{:S(2)}, u32[]{:S(2)}) collective-permute-start(f32[8,128]{1,0:T(8,128)} %peak.1.refs_0_), channel_id=1, source_target_pairs={{0,3},{1,4},{2,5},{3,6},{4,7},{5,0},{6,1},{7,2},{8,11},{9,12},{10,... | collective-permute-start | bytes 12296 | tf_op jit(solution)/shard_map/ppermute | solution.py:239
  72.8 10.4 %collective-permute-start.3 = (f32[8,128]{1,0:T(8,128)}, f32[8,128]{1,0:T(8,128)S(1)}, u32[]{:S(2)}, u32[]{:S(2)}) collective-permute-start(f32[8,128]{1,0:T(8,128)} %peak.1.refs_0_), channel_id=1, source_target_pairs={{0,4},{1,5},{2,6},{3,7},{4,0},{5,1},{6,2},{7,3},{8,12},{9,13},{10,... | collective-permute-start | bytes 12296 | tf_op jit(solution)/shard_map/ppermute | solution.py:239
  72.8 10.5 %collective-permute-start.4 = (f32[8,128]{1,0:T(8,128)}, f32[8,128]{1,0:T(8,128)S(1)}, u32[]{:S(2)}, u32[]{:S(2)}) collective-permute-start(f32[8,128]{1,0:T(8,128)} %peak.1.refs_0_), channel_id=1, source_target_pairs={{0,5},{1,6},{2,7},{3,0},{4,1},{5,2},{6,3},{7,4},{8,13},{9,14},{10,... | collective-permute-start | bytes 12296 | tf_op jit(solution)/shard_map/ppermute | solution.py:239
  76.3 6.2 %copy-start.4 = (f32[8,128]{1,0:T(8,128)}, f32[8,128]{1,0:T(8,128)S(1)}, u32[]{:S(2)}) copy-start(f32[8,128]{1,0:T(8,128)S(1)} %collective-permute-done.refs_1_) | copy-start | bytes 12292
  76.3 6.9 %collective-permute-start.5 = (f32[8,128]{1,0:T(8,128)}, f32[8,128]{1,0:T(8,128)S(1)}, u32[]{:S(2)}, u32[]{:S(2)}) collective-permute-start(f32[8,128]{1,0:T(8,128)} %peak.1.refs_0_), channel_id=1, source_target_pairs={{0,6},{1,7},{2,0},{3,1},{4,2},{5,3},{6,4},{7,5},{8,14},{9,15},{10,... | collective-permute-start | bytes 12296 | tf_op jit(solution)/shard_map/ppermute | solution.py:239
  79.5 3.0 %copy-start.5 = (f32[8,128]{1,0:T(8,128)}, f32[8,128]{1,0:T(8,128)S(1)}, u32[]{:S(2)}) copy-start(f32[8,128]{1,0:T(8,128)S(1)} %collective-permute-done.1.refs_2_) | copy-start | bytes 12292
  79.5 3.8 %collective-permute-start.6 = (f32[8,128]{1,0:T(8,128)}, f32[8,128]{1,0:T(8,128)S(1)}, u32[]{:S(2)}, u32[]{:S(2)}) collective-permute-start(f32[8,128]{1,0:T(8,128)} %peak.1.refs_0_), channel_id=1, source_target_pairs={{0,7},{1,0},{2,1},{3,2},{4,3},{5,4},{6,5},{7,6},{8,15},{9,8},{10,9... | collective-permute-start | bytes 12296 | tf_op jit(solution)/shard_map/ppermute | solution.py:239
  83.2 0.6 copy-start.6
  83.2 0.6 copy-start.7
  83.2 0.6 copy-start.8
  83.3 0.6 copy-start.9
  83.9 0.6 copy-start.10
where the time goes:
time: 90.9 us; the launch traced here: 90.1 us
  waiting for transfers between devices  31.6 us (35%)
  starting transfers between devices  30.5 us (34%)
  Pallas kernels  19 us (21%)
  local copies, waits for them, and re-layouts  7.57 us (8%)
    ppermute x7, starting transfers between devices, shards(): lax.ppermute(peak, 'ch', [(i, (i + by) % ch) for i in range(ch)])  17.2 us
    all_to_all x1, waiting for transfers between devices, shards(): lax.all_to_all(gated, 'ctx', split_axis=0, concat_axis=0, tiled=True)  15.8 us
    all_to_all x1, waiting for transfers between devices, shards(): lax.all_to_all(y.reshape(channels, 2 * rows), 'ctx', split_axis=0, concat...  15.6 us
    pallas_call x1, Pallas kernels, shards(): pl.pallas_call(conv_kernel, grid=(mine,), in_specs=[pl.BlockSpec((1, 1, t...  7.08 us
    all_to_all x1, starting transfers between devices, shards(): lax.all_to_all(gated, 'ctx', split_axis=0, concat_axis=0, tiled=True)  6.01 us
    unnamed x25, local copies, waits for them, and re-layouts  4.9 us
    pallas_call x1, Pallas kernels, shards(): pl.pallas_call(functools.partial(scale_kernel, block=block), grid=steps,...  4.23 us
    pallas_call x1, Pallas kernels, shards(): pl.pallas_call(functools.partial(gate_kernel, block=block), grid=steps, i...  4.07 us
  transfers between devices with their start and end apart: 10, of which 3 were waited for; matrix products, arithmetic and copies ran while one was open for 4% of the time, Pallas kernels for 4%

commit v1 on v0

--- a/solution.py
+++ b/solution.py
@@ -11,8 +11,13 @@
 TILE = 128
 
 
-def power(exponent):
-    return lax.shift_left(jnp.int32(1), exponent + 8).astype(jnp.float32) * (2.0 ** -8)
+def power(e_ref, i, b, p):
+    exponent = e_ref[i]
+    rows = lax.broadcasted_iota(jnp.int32, exponent.shape, 0)
+    lanes = lax.broadcasted_iota(jnp.int32, exponent.shape, 1)
+    value = lax.shift_left(jnp.ones_like(exponent), exponent + 8).astype(jnp.float32) * (2.0 ** -8)
+    value = jnp.where((rows == p) & (lanes == b), value, 0.0)
+    return jnp.sum(jnp.sum(value, axis=0, keepdims=True), axis=1, keepdims=True)
 
 
 def mirror():
@@ -43,6 +48,8 @@
 
 
 PARTS = 2
+TERMS = 3
+EXTRA = 8
 
 
 def gate_kernel(e_ref, q_ref, k_ref, v_ref, g_ref, out_ref, *, block):
@@ -50,9 +57,9 @@
     flip = mirror()
     for n, p, at, lanes in squares(q_ref, block):
         b = first + n
-        q_real = q_ref[at, lanes].astype(jnp.float32) * power(e_ref[0, b, p])
-        k_real = k_ref[at, lanes].astype(jnp.float32) * power(e_ref[1, b, p])
-        v_real = v_ref[at, lanes].astype(jnp.float32) * power(e_ref[2, b, p])
+        q_real = q_ref[at, lanes].astype(jnp.float32) * power(e_ref, 0, b, p)
+        k_real = k_ref[at, lanes].astype(jnp.float32) * power(e_ref, 1, b, p)
+        v_real = v_ref[at, lanes].astype(jnp.float32) * power(e_ref, 2, b, p)
         out_ref[at, lanes] = (k_real * v_real).astype(jnp.bfloat16)
         gw = (q_real * g_ref[at, lanes].astype(jnp.float32)).astype(jnp.bfloat16)
         o = 2 * PARTS - 1 - p
@@ -61,8 +68,9 @@
         ).astype(jnp.bfloat16)
 
 
-def conv_kernel(taps_ref, x_ref, y_ref, lag_ref, toe_ref, z_ref, u_ref, b_ref):
-    blocks, width = x_ref.shape[:2]
+def conv_kernel(taps_ref, x_ref, y_ref, toe_ref, z_ref, u_ref, b_ref, lag_ref, *, width):
+    blocks, part = x_ref.shape[:2]
+    own = pl.ds(pl.multiple_of(pl.program_id(0) * width, width), width)
     taps = taps_ref.shape[2]
     span = taps + TILE
     tiles = span // TILE
@@ -82,12 +90,12 @@
 
     def z_tile(t):
         t = t % count
-        return x_ref[t // PARTS, :, (t % PARTS) * TILE : (t % PARTS + 1) * TILE]
+        return x_ref[t // PARTS, own, (t % PARTS) * TILE : (t % PARTS + 1) * TILE]
 
     def back_tile(t):
         t = t % count
         o = PARTS + t % PARTS
-        return x_ref[blocks - 1 - t // PARTS, :, o * TILE : (o + 1) * TILE]
+        return x_ref[blocks - 1 - t // PARTS, own, o * TILE : (o + 1) * TILE]
 
     for n in range(count + lead):
         rows = slice(n * width, (n + 1) * width)
@@ -102,13 +110,13 @@
 
     w = jnp.dot(window(z_ref), toe_ref[...], preferred_element_type=jnp.float32)
     for t in range(count):
-        y_ref[t // PARTS, :, (t % PARTS) * TILE : (t % PARTS + 1) * TILE] = w[
+        y_ref[t // PARTS, own, (t % PARTS) * TILE : (t % PARTS + 1) * TILE] = w[
             t * width : (t + 1) * width, :
         ].astype(jnp.bfloat16)
     gz = jnp.dot(window(b_ref), toe_ref[...], preferred_element_type=jnp.float32)
     for t in range(count):
         o = PARTS + t % PARTS
-        y_ref[blocks - 1 - t // PARTS, :, o * TILE : (o + 1) * TILE] = gz[
+        y_ref[blocks - 1 - t // PARTS, own, o * TILE : (o + 1) * TILE] = gz[
             t * width : (t + 1) * width, :
         ].astype(jnp.bfloat16)
 
@@ -128,27 +136,46 @@
     pieces = taps // TILE
     stacked = jnp.concatenate([diag[:, n * TILE : (n + 1) * TILE] for n in range(pieces)], axis=0)
     stacked = mirrored(stacked, mirror(), 3)
-    for n in range(pieces):
-        o = pieces - 1 - n
-        lag_ref[0, o : o + 1, :] = stacked[n : n + 1, :]
+    share = lag_ref.shape[2]
+    mine = pl.ds(pl.program_id(0), 1)
+    for r in range(blocks):
+        n = pieces - 1 - r * share // TILE
+        at = r * share % TILE
+        lag_ref[r, mine, :] = stacked[n : n + 1, at : at + share]
+
+    @pl.when(pl.program_id(0) == 0)
+    def _():
+        y_ref[:, part:, :] = jnp.zeros((blocks, y_ref.shape[1] - part, y_ref.shape[2]), jnp.bfloat16)
+
+    @pl.when(pl.program_id(0) == pl.num_programs(0) - 1)
+    def _():
+        rest = lag_ref[...]
+        for term in range(TERMS):
+            piece = rest.astype(jnp.bfloat16)
+            y_ref[:, part : part + rest.shape[1], term * TILE : term * TILE + share] = piece
+            rest = rest - piece.astype(jnp.float32)
 
 
 def gradients(e_ref, k_ref, v_ref, g_ref, y_ref, block):
     first = pl.program_id(0) * (k_ref.shape[0] // block)
+    part = y_ref.shape[1] - EXTRA
+    each = block // part
     flip = mirror()
     for n, p, at, lanes in squares(k_ref, block):
         o = 2 * PARTS - 1 - p
-        w = y_ref[at, lanes].astype(jnp.float32)
-        gz = jnp.dot(
-            y_ref[at, o * TILE : (o + 1) * TILE], flip, preferred_element_type=jnp.float32
+        senders = range(n * each, (n + 1) * each)
+        w = jnp.concatenate([y_ref[s, :part, lanes] for s in senders], axis=0).astype(jnp.float32)
+        back = jnp.concatenate(
+            [y_ref[s, :part, o * TILE : (o + 1) * TILE] for s in senders], axis=0
         )
-        v_real = v_ref[at, lanes].astype(jnp.float32) * power(e_ref[2, first + n, p])
-        k_real = k_ref[at, lanes].astype(jnp.float32) * power(e_ref[1, first + n, p])
+        gz = jnp.dot(back, flip, preferred_element_type=jnp.float32)
+        v_real = v_ref[at, lanes].astype(jnp.float32) * power(e_ref, 2, first + n, p)
+        k_real = k_ref[at, lanes].astype(jnp.float32) * power(e_ref, 1, first + n, p)
         g = g_ref[at, lanes].astype(jnp.float32)
         yield p, at, lanes, (g * w, gz * v_real, gz * k_real)
 
 
-def peak_kernel(e_ref, k_ref, v_ref, g_ref, y_ref, peak_ref, *, block):
+def peak_kernel(e_ref, k_ref, v_ref, g_ref, y_ref, out_ref, peak_ref, *, block):
     @pl.when(pl.program_id(0) == 0)
     def _():
         peak_ref[...] = jnp.zeros(peak_ref.shape, jnp.float32)
@@ -161,16 +188,25 @@
 
     @pl.when(pl.program_id(0) == pl.num_programs(0) - 1)
     def _():
-        best = jnp.max(peak_ref[...], axis=1, keepdims=True)
-        peak_ref[...] = jnp.broadcast_to(best, peak_ref.shape)
-
-
-def scale_kernel(e_ref, k_ref, v_ref, g_ref, y_ref, *refs, block):
-    peaks, (oq_ref, ok_ref, ov_ref, top_ref) = refs[:-4], refs[-4:]
-    top = peaks[0][...]
-    for ref in peaks[1:]:
-        top = jnp.maximum(top, ref[...])
-    top_ref[...] = top
+        for n in range(out_ref.shape[0]):
+            out_ref[n] = peak_ref[...]
+
+
+def scale_kernel(e_ref, k_ref, v_ref, g_ref, y_ref, peaks_ref, oq_ref, ok_ref, ov_ref, lag_ref, top_ref, *, block):
+    top = jnp.max(peaks_ref[...], axis=0)
+    for p in range(PARTS):
+        for i in range(3):
+            best = jnp.max(top[p * 4 + i : p * 4 + i + 1, :], axis=1, keepdims=True)
+            top_ref[p : p + 1, i : i + 1] = best
+    top = jnp.max(top, axis=1, keepdims=True)
+    part = y_ref.shape[1] - EXTRA
+    share = lag_ref.shape[1]
+    mine = lag_ref.shape[0] // y_ref.shape[0]
+    for s in range(y_ref.shape[0]):
+        terms = [
+            y_ref[s, part:, t * TILE : t * TILE + share].astype(jnp.float32) for t in range(TERMS)
+        ]
+        lag_ref[s * mine : (s + 1) * mine, :] = (terms[0] + (terms[1] + terms[2]))[:mine, :]
     inverse = 1.0 / (top + EPS)
     for p, at, lanes, products in gradients(e_ref, k_ref, v_ref, g_ref, y_ref, block):
         for i, (product, ref) in enumerate(zip(products, (oq_ref, ok_ref, ov_ref))):
@@ -189,10 +225,10 @@
     span = taps + TILE
     tall = 2 * block
     steps = (channels // tall,)
-    scalars = pl.BlockSpec(memory_space=pltpu.SMEM)
+    exponents = exponents.transpose(0, 2, 1)
+    scalars = pl.BlockSpec(exponents.shape, lambda b: (0, 0, 0))
     tile = pl.BlockSpec((tall, rows), lambda b: (b, 0))
     double = pl.BlockSpec((tall, 2 * rows), lambda b: (b, 0))
-    whole = pl.BlockSpec((8, TILE), lambda b: (0, 0))
     bf16 = jnp.bfloat16
 
     gated = pl.pallas_call(
@@ -207,48 +243,54 @@
 
     own_taps = lax.dynamic_slice_in_dim(filter_taps, lax.axis_index("ctx") * mine, mine, 0)
     stack = pltpu.VMEM(((ctx * PARTS + taps // TILE) * width, TILE), bf16)
-    seq = pl.BlockSpec((ctx, width, 2 * rows), lambda b: (0, b, 0))
-    y, lag = pl.pallas_call(
-        conv_kernel,
+    resident = pl.BlockSpec(memory_space=pltpu.VMEM)
+    y = pl.pallas_call(
+        functools.partial(conv_kernel, width=width),
         grid=(mine,),
-        in_specs=[pl.BlockSpec((1, 1, taps), lambda b: (b, 0, 0)), seq],
-        out_specs=[seq, pl.BlockSpec((1, taps // TILE, TILE), lambda b: (b, 0, 0))],
-        out_shape=[
-            jax.ShapeDtypeStruct((ctx, part, 2 * rows), bf16),
-            jax.ShapeDtypeStruct((mine, taps // TILE, TILE), jnp.float32),
+        in_specs=[pl.BlockSpec((1, 1, taps), lambda b: (b, 0, 0)), resident],
+        out_specs=resident,
+        out_shape=jax.ShapeDtypeStruct((ctx, part + EXTRA, 2 * rows), bf16),
+        scratch_shapes=[
+            pltpu.VMEM((span, TILE), bf16),
+            stack,
+            stack,
+            stack,
+            pltpu.VMEM((ctx, EXTRA, taps // ctx), jnp.float32),
         ],
-        scratch_shapes=[pltpu.VMEM((span, TILE), bf16), stack, stack, stack],
         name="conv",
     )(own_taps.reshape(mine, 1, taps), swapped.reshape(ctx, part, 2 * rows))
 
-    y = lax.all_to_all(y.reshape(channels, 2 * rows), "ctx", split_axis=0, concat_axis=0, tiled=True)
-    pieces = lag.reshape(mine, ctx, taps // ctx).transpose(1, 0, 2)
-    pieces = lax.all_to_all(pieces, "ctx", split_axis=0, concat_axis=0, tiled=True)
-    grad_filter = pieces.reshape(groups, taps // ctx)
-
-    peak = pl.pallas_call(
+    y = lax.all_to_all(y, "ctx", split_axis=0, concat_axis=0, tiled=True)
+    mixed = pl.BlockSpec((tall // part, part + EXTRA, 2 * rows), lambda b: (b, 0, 0))
+    every = pl.BlockSpec((ch, 8, TILE), lambda b: (0, 0, 0))
+    peaks = pl.pallas_call(
         functools.partial(peak_kernel, block=block),
         grid=steps,
-        in_specs=[scalars] + [tile] * 3 + [double],
-        out_specs=whole,
-        out_shape=jax.ShapeDtypeStruct((8, TILE), jnp.float32),
+        in_specs=[scalars] + [tile] * 3 + [mixed],
+        out_specs=every,
+        out_shape=jax.ShapeDtypeStruct((ch, 8, TILE), jnp.float32),
+        scratch_shapes=[pltpu.VMEM((8, TILE), jnp.float32)],
         name="peak",
     )(exponents, k_vals, v_vals, grad_out, y)
-    peaks = [peak]
-    for by in range(1, ch):
-        peaks.append(lax.ppermute(peak, "ch", [(i, (i + by) % ch) for i in range(ch)]))
-
-    oq, ok, ov, top = pl.pallas_call(
+    peaks = lax.all_to_all(peaks, "ch", split_axis=0, concat_axis=0, tiled=True)
+
+    oq, ok, ov, grad_filter, top = pl.pallas_call(
         functools.partial(scale_kernel, block=block),
         grid=steps,
-        in_specs=[scalars] + [tile] * 3 + [double] + [whole] * ch,
-        out_specs=[tile] * 3 + [whole],
+        in_specs=[scalars] + [tile] * 3 + [mixed, every],
+        out_specs=[tile] * 3
+        + [
+            pl.BlockSpec((groups // steps[0], taps // ctx), lambda b: (b, 0)),
+            pl.BlockSpec((PARTS, 3), lambda b: (0, 0)),
+        ],
         out_shape=[jax.ShapeDtypeStruct((channels, rows), bf16)] * 3
-        + [jax.ShapeDtypeStruct((8, TILE), jnp.float32)],
+        + [
+            jax.ShapeDtypeStruct((groups, taps // ctx), jnp.float32),
+            jax.ShapeDtypeStruct((PARTS, 3), jnp.float32),
+        ],
         name="scale",
-    )(exponents, k_vals, v_vals, grad_out, y, *peaks)
-    block_peak = top[:, 0].reshape(PARTS, 4)[:, :3].T
-    return oq, ok, ov, grad_filter, block_peak
+    )(exponents, k_vals, v_vals, grad_out, y, peaks)
+    return oq, ok, ov, grad_filter, top.T
 
 
 def solution(mesh):

time: 90.9 us -> 81.9 us (0.901)
  blocking collectives: 0 us -> 37.2 us
  starting transfers between devices: 30.5 us -> 6.01 us
  waiting for transfers between devices: 31.6 us -> 15.8 us
  local copies, waits for them, and re-layouts: 7.57 us -> 1.64 us
  Pallas kernels: 19 us -> 20 us
    all_to_all x0 -> x2, blocking collectives: none -> 37.2 us  [the longest x1 22 us: shards(): y = lax.all_to_all(y, 'ctx', split_axis=0, concat_axis=0, tiled=True)]
    ppermute x7 -> x0, starting transfers between devices: 17.2 us -> none  [shards(): lax.ppermute(peak, 'ch', [(i, (i + by) % ch) for i in range(ch)])]
    all_to_all x2 -> x0, waiting for transfers between devices: 15.6 us -> none  [the longest x1 15.6 us: shards(): lax.all_to_all(y.reshape(channels, 2 * rows), 'ctx', split_axis=0, concat...]
    all_to_all x2 -> x0, starting transfers between devices: 7.28 us -> none  [the longest x1 3.78 us: shards(): lax.all_to_all(y.reshape(channels, 2 * rows), 'ctx', split_axis=0, concat...]
    unnamed x25 -> x4, local copies, waits for them, and re-layouts: 4.9 us -> 1.01 us
  transfers between devices with their start and end apart: 10 -> 1, of which waited for: 3 -> 1; matrix products, arithmetic and copies ran while one was open for 4% -> 1% of each run, Pallas kernels for 4% -> 0%
where the time goes in v1:
time: 81.9 us; the launch traced here: 81.4 us
  blocking collectives  37.2 us (45%)
  Pallas kernels  20 us (24%)
  waiting for transfers between devices  15.8 us (19%)
  starting transfers between devices  6.01 us (7%)
  local copies, waits for them, and re-layouts  1.64 us (2%)
    all_to_all x1, blocking collectives, shards(): y = lax.all_to_all(y, 'ctx', split_axis=0, concat_axis=0, tiled=True)  22 us
    all_to_all x1, waiting for transfers between devices, shards(): lax.all_to_all(gated, 'ctx', split_axis=0, concat_axis=0, tiled=True)  15.8 us
    all_to_all x1, blocking collectives, shards(): peaks = lax.all_to_all(peaks, 'ch', split_axis=0, concat_axis=0, tiled=True)  15.2 us
    pallas_call x1, Pallas kernels, shards(): pl.pallas_call(functools.partial(conv_kernel, width=width), grid=(mine,),...  7.94 us
    all_to_all x1, starting transfers between devices, shards(): lax.all_to_all(gated, 'ctx', split_axis=0, concat_axis=0, tiled=True)  6.01 us
    pallas_call x1, Pallas kernels, shards(): pl.pallas_call(functools.partial(scale_kernel, block=block), grid=steps,...  4.27 us
    pallas_call x1, Pallas kernels, shards(): pl.pallas_call(functools.partial(gate_kernel, block=block), grid=steps, i...  4.14 us
    pallas_call x1, Pallas kernels, shards(): pl.pallas_call(functools.partial(peak_kernel, block=block), grid=steps, i...  3.63 us
  transfers between devices with their start and end apart: 1, of which 1 were waited for; matrix products, arithmetic and copies ran while one was open for 1% of the time, Pallas kernels for 0%

profile of v1, /device:TPU:0, one launch (start us, length us, event | category | flops | bytes accessed | tf_op | source)
XLA Modules:
  0.0 81.4 jit_solution(10807016984661053669)
XLA Ops:
  0.6 0.0 copy-start
  0.6 4.1 %gate.1 = bf16[1024,512]{1,0:T(8,128)(2,1)} custom-call(s32[3,2,8]{2,1,0:T(2,128)} %bitcast.4, bf16[1024,256]{1,0:T(8,128)(2,1)} %q_ref.1, bf16[1024,256]{1,0:T(8,128)(2,1)} %k_ref.5, bf16[1024,256]{1,0:T(8,128)(2,1)} %v_ref.5, bf16[1024,256]{1,0:T(8,128)(2,1)} %g_ref.5), custom_call_target="tpu_custom_call" | custom-call | tf_op jit(solution)/shard_map/gate/pallas_call | solution.py:234
  4.8 6.0 %all-to-all-start = ((bf16[16,64,512]{2,1,0:T(8,128)(2,1)}), bf16[16,64,512]{2,1,0:T(8,128)(2,1)S(1)}, u32[]{:S(2)}, u32[]{:S(2)}) async-start(bf16[16,64,512]{2,1,0:T(8,128)(2,1)} %bitcast.3), calls=%async_computation | async-start | bytes 2097152 | tf_op jit(solution)/shard_map/all_to_all | solution.py:242
  10.8 0.0 copy-done
  10.8 0.6 reshape.17.taps_ref
  11.5 15.8 %all-to-all-done.x_ref = bf16[16,64,512]{2,1,0:T(8,128)(2,1)S(1)} async-done(((bf16[16,64,512]{2,1,0:T(8,128)(2,1)}), bf16[16,64,512]{2,1,0:T(8,128)(2,1)S(1)}, u32[]{:S(2)}, u32[]{:S(2)}) %all-to-all-start) | async-done | bytes 1048608 | tf_op jit(solution)/shard_map/all_to_all | solution.py:242
  27.3 0.0 copy-start.1
  27.3 1.0 %copy-done.1 = bf16[16,64,512]{2,1,0:T(8,128)(2,1)} copy-done((bf16[16,64,512]{2,1,0:T(8,128)(2,1)}, bf16[16,64,512]{2,1,0:T(8,128)(2,1)S(1)}, u32[]{:S(2)}) %copy-start.1) | copy-done | bytes 1048600
  28.3 7.9 %conv.1 = bf16[16,72,512]{2,1,0:T(8,128)(2,1)} custom-call(f32[4,1,1024]{2,1,0:T(1,128)} %reshape.17.taps_ref, bf16[16,64,512]{2,1,0:T(8,128)(2,1)} %copy-done.1), custom_call_target="tpu_custom_call" | custom-call | tf_op jit(solution)/shard_map/conv/pallas_call | solution.py:247
  36.2 22.0 %all_to_all.19.y_ref = bf16[16,72,512]{2,1,0:T(8,128)(2,1)} all-to-all(bf16[16,72,512]{2,1,0:T(8,128)(2,1)} %conv.1), channel_id=1, replica_groups=mesh['ctx'=16,'ch'=8] {'ctx'}, dimensions={0} | all-to-all | bytes 2359296 | tf_op jit(solution)/shard_map/all_to_all | solution.py:263
  58.3 3.6 %peak.1 = f32[8,8,128]{2,1,0:T(8,128)} custom-call(s32[3,2,8]{2,1,0:T(2,128)} %bitcast.5, bf16[1024,256]{1,0:T(8,128)(2,1)} %k_ref.5, bf16[1024,256]{1,0:T(8,128)(2,1)} %v_ref.5, bf16[1024,256]{1,0:T(8,128)(2,1)} %g_ref.5, bf16[16,72,512]{2,1,0:T(8,128)(2,1)} %all_to_all.19.y_ref), custom_call_target="tpu_custom_call" | custom-call | tf_op jit(solution)/shard_map/peak/pallas_call | solution.py:266
  61.9 15.2 %all_to_all.20.peaks_ref = f32[8,8,128]{2,1,0:T(8,128)} all-to-all(f32[8,8,128]{2,1,0:T(8,128)} %peak.1), channel_id=1, replica_groups=mesh['ctx'=16,'ch'=8] {'ch'}, dimensions={0} | all-to-all | bytes 65536 | tf_op jit(solution)/shard_map/all_to_all | solution.py:275
  77.1 4.3 %scale.1 = (bf16[1024,256]{1,0:T(8,128)(2,1)}, bf16[1024,256]{1,0:T(8,128)(2,1)}, bf16[1024,256]{1,0:T(8,128)(2,1)}, f32[64,64]{1,0:T(8,128)}, f32[2,3]{1,0:T(2,128)}) custom-call(s32[3,2,8]{2,1,0:T(2,128)} %bitcast.6, bf16[1024,256]{1,0:T(8,128)(2,1)} %k_ref.5, bf16[1024,256]{1,0:T(8,128)(2,1)} %v_ref.5, bf16[1024,256]{1,0:T(8,128)(2,1)} %g_ref.5, ...), custom_call_target="tpu_custom_call" | custom-call | tf_op jit(solution)/shard_map/scale/pallas_call | solution.py:277
  (1 shorter events, 0.0 us)
Async XLA Ops:
  0.6 10.2 %copy-start = (f32[64,1024]{1,0:T(8,128)S(1)}, f32[64,1024]{1,0:T(8,128)}, u32[]{:S(2)}) copy-start(f32[64,1024]{1,0:T(8,128)} %param.11) | copy-start | bytes 786436
  4.8 22.5 %all-to-all-start = ((bf16[16,64,512]{2,1,0:T(8,128)(2,1)}), bf16[16,64,512]{2,1,0:T(8,128)(2,1)S(1)}, u32[]{:S(2)}, u32[]{:S(2)}) async-start(bf16[16,64,512]{2,1,0:T(8,128)(2,1)} %bitcast.3), calls=%async_computation | async-start | bytes 2097152 | tf_op jit(solution)/shard_map/all_to_all | solution.py:242
  27.3 1.0 %copy-start.1 = (bf16[16,64,512]{2,1,0:T(8,128)(2,1)}, bf16[16,64,512]{2,1,0:T(8,128)(2,1)S(1)}, u32[]{:S(2)}) copy-start(bf16[16,64,512]{2,1,0:T(8,128)(2,1)S(1)} %all-to-all-done.x_ref) | copy-start | bytes 3145732

commit v2 on v1

--- a/solution.py
+++ b/solution.py
@@ -68,25 +68,44 @@
         ).astype(jnp.bfloat16)
 
 
-def conv_kernel(taps_ref, x_ref, y_ref, toe_ref, z_ref, u_ref, b_ref, lag_ref, *, width):
-    blocks, part = x_ref.shape[:2]
-    own = pl.ds(pl.multiple_of(pl.program_id(0) * width, width), width)
-    taps = taps_ref.shape[2]
+def conv_kernel(taps_ref, x_ref, y_ref, lag_ref, *scratch, width):
+    blocks, part, lanes = x_ref.shape
+    groups, taps = taps_ref.shape
+    y_ref[:, part:, :] = jnp.zeros((blocks, y_ref.shape[1] - part, lanes), jnp.bfloat16)
+    each = len(scratch) // groups
+    for g in range(groups):
+        one_group(g, taps_ref, x_ref, y_ref, lag_ref, *scratch[g * each : (g + 1) * each], width)
+    rest = lag_ref[...]
+    for term in range(TERMS):
+        piece = rest.astype(jnp.bfloat16)
+        y_ref[:, part : part + rest.shape[1], term * TILE : term * TILE + rest.shape[2]] = piece
+        rest = rest - piece.astype(jnp.float32)
+
+
+def one_group(g, taps_ref, x_ref, y_ref, lag_ref, toe_ref, z_ref, b_ref, own_ref, u_ref, width):
+    blocks = x_ref.shape[0]
+    taps = taps_ref.shape[1]
     span = taps + TILE
     tiles = span // TILE
     lead = tiles - 1
     count = blocks * PARTS
-
-    row = taps_ref[0].astype(jnp.bfloat16).astype(jnp.float32)
+    own = slice(g * width, (g + 1) * width)
+
+    row = taps_ref[g : g + 1, :].astype(jnp.bfloat16).astype(jnp.float32)
     row = jnp.concatenate([row, jnp.zeros((1, TILE), jnp.float32)], axis=1)
     row = jnp.broadcast_to(row, (8, span))
     low = pltpu.roll(row, 0, 1, stride=1, stride_axis=0)
     high = pltpu.roll(row, 8, 1, stride=1, stride_axis=0)
     base = jnp.concatenate([low, high], axis=0).astype(jnp.bfloat16)
+    blank = jnp.zeros((TILE, TILE), jnp.bfloat16)
+    toe_ref[0:TILE, 0:TILE] = blank
+    toe_ref[tiles * TILE : (tiles + 1) * TILE, TILE : 2 * TILE] = blank
     for a in range(0, TILE, 16):
         rolled = pltpu.roll(base, a, 1) if a else base
         for d in range(tiles):
-            toe_ref[d * TILE + a : d * TILE + a + 16, :] = rolled[:, d * TILE : (d + 1) * TILE]
+            piece = rolled[:, d * TILE : (d + 1) * TILE]
+            toe_ref[(d + 1) * TILE + a : (d + 1) * TILE + a + 16, 0:TILE] = piece
+            toe_ref[d * TILE + a : d * TILE + a + 16, TILE : 2 * TILE] = piece
 
     def z_tile(t):
         t = t % count
@@ -97,34 +116,37 @@
         o = PARTS + t % PARTS
         return x_ref[blocks - 1 - t // PARTS, own, o * TILE : (o + 1) * TILE]
 
+    half = lead // 2
+    for m in range(blocks + half):
+        rows = slice(m * width, (m + 1) * width)
+        for p in range(2):
+            lanes = slice((1 - p) * TILE, (2 - p) * TILE)
+            z_ref[rows, lanes] = z_tile(2 * (m - half) + p)
+            b_ref[rows, lanes] = back_tile(2 * (m - half) + p)
+    for n in range(count):
+        own_ref[n * width : (n + 1) * width, :] = back_tile(n)
     for n in range(count + lead):
-        rows = slice(n * width, (n + 1) * width)
-        z_ref[rows, :] = z_tile(n - lead)
-        b_ref[rows, :] = back_tile(n - lead)
-        u_ref[rows, :] = z_tile(count - 1 - n)
+        u_ref[n * width : (n + 1) * width, :] = z_tile(count - 1 - n)
 
     def window(ref):
         return jnp.concatenate(
-            [ref[(lead - d) * width : (lead - d + count) * width, :] for d in range(tiles)], axis=1
+            [ref[(half - f) * width : (half - f + blocks) * width, :] for f in range(half + 1)], axis=1
         )
 
     w = jnp.dot(window(z_ref), toe_ref[...], preferred_element_type=jnp.float32)
-    for t in range(count):
-        y_ref[t // PARTS, own, (t % PARTS) * TILE : (t % PARTS + 1) * TILE] = w[
-            t * width : (t + 1) * width, :
-        ].astype(jnp.bfloat16)
+    for n in range(blocks):
+        y_ref[n, own, 0 : 2 * TILE] = w[n * width : (n + 1) * width, :].astype(jnp.bfloat16)
     gz = jnp.dot(window(b_ref), toe_ref[...], preferred_element_type=jnp.float32)
-    for t in range(count):
-        o = PARTS + t % PARTS
-        y_ref[blocks - 1 - t // PARTS, own, o * TILE : (o + 1) * TILE] = gz[
-            t * width : (t + 1) * width, :
-        ].astype(jnp.bfloat16)
-
+    for n in range(blocks):
+        y_ref[blocks - 1 - n, own, 2 * TILE : 4 * TILE] = gz[n * width : (n + 1) * width, :].astype(
+            jnp.bfloat16
+        )
+
+    shifted = jnp.concatenate(
+        [u_ref[(lead - d) * width : (lead - d + count) * width, :] for d in range(tiles)], axis=1
+    )
     cross = lax.dot_general(
-        b_ref[lead * width : (lead + count) * width, :],
-        window(u_ref),
-        (((0,), (0,)), ((), ())),
-        preferred_element_type=jnp.float32,
+        own_ref[...], shifted, (((0,), (0,)), ((), ())), preferred_element_type=jnp.float32
     )
     total = None
     for a in range(0, TILE, 8):
@@ -137,23 +159,10 @@
     stacked = jnp.concatenate([diag[:, n * TILE : (n + 1) * TILE] for n in range(pieces)], axis=0)
     stacked = mirrored(stacked, mirror(), 3)
     share = lag_ref.shape[2]
-    mine = pl.ds(pl.program_id(0), 1)
     for r in range(blocks):
         n = pieces - 1 - r * share // TILE
         at = r * share % TILE
-        lag_ref[r, mine, :] = stacked[n : n + 1, at : at + share]
-
-    @pl.when(pl.program_id(0) == 0)
-    def _():
-        y_ref[:, part:, :] = jnp.zeros((blocks, y_ref.shape[1] - part, y_ref.shape[2]), jnp.bfloat16)
-
-    @pl.when(pl.program_id(0) == pl.num_programs(0) - 1)
-    def _():
-        rest = lag_ref[...]
-        for term in range(TERMS):
-            piece = rest.astype(jnp.bfloat16)
-            y_ref[:, part : part + rest.shape[1], term * TILE : term * TILE + share] = piece
-            rest = rest - piece.astype(jnp.float32)
+        lag_ref[r, g : g + 1, :] = stacked[n : n + 1, at : at + share]
 
 
 def gradients(e_ref, k_ref, v_ref, g_ref, y_ref, block):
@@ -242,23 +251,25 @@
     swapped = lax.all_to_all(gated, "ctx", split_axis=0, concat_axis=0, tiled=True)
 
     own_taps = lax.dynamic_slice_in_dim(filter_taps, lax.axis_index("ctx") * mine, mine, 0)
-    stack = pltpu.VMEM(((ctx * PARTS + taps // TILE) * width, TILE), bf16)
+    count = ctx * PARTS
+    lead = taps // TILE
+    pair = pltpu.VMEM(((ctx + lead // 2) * width, 2 * TILE), bf16)
+    scratch = [
+        pltpu.VMEM((span + TILE, 2 * TILE), bf16),
+        pair,
+        pair,
+        pltpu.VMEM((count * width, TILE), bf16),
+        pltpu.VMEM(((count + lead) * width, TILE), bf16),
+    ]
     resident = pl.BlockSpec(memory_space=pltpu.VMEM)
     y = pl.pallas_call(
         functools.partial(conv_kernel, width=width),
-        grid=(mine,),
-        in_specs=[pl.BlockSpec((1, 1, taps), lambda b: (b, 0, 0)), resident],
+        in_specs=[resident, resident],
         out_specs=resident,
         out_shape=jax.ShapeDtypeStruct((ctx, part + EXTRA, 2 * rows), bf16),
-        scratch_shapes=[
-            pltpu.VMEM((span, TILE), bf16),
-            stack,
-            stack,
-            stack,
-            pltpu.VMEM((ctx, EXTRA, taps // ctx), jnp.float32),
-        ],
+        scratch_shapes=[pltpu.VMEM((ctx, EXTRA, taps // ctx), jnp.float32)] + scratch * mine,
         name="conv",
-    )(own_taps.reshape(mine, 1, taps), swapped.reshape(ctx, part, 2 * rows))
+    )(own_taps, pltpu.with_memory_space_constraint(swapped.reshape(ctx, part, 2 * rows), pltpu.VMEM))
 
     y = lax.all_to_all(y, "ctx", split_axis=0, concat_axis=0, tiled=True)
     mixed = pl.BlockSpec((tall // part, part + EXTRA, 2 * rows), lambda b: (b, 0, 0))

time: 81.9 us -> 78.7 us (0.961)
  Pallas kernels: 20 us -> 17.7 us
  local copies, waits for them, and re-layouts: 1.64 us -> 0.62 us
    pallas_call x1, Pallas kernels: 7.94 us -> 5.7 us  [shards(): pl.pallas_call(functools.partial(conv_kernel, width=width), in_specs=[res...]
    unnamed x4 -> x2, local copies, waits for them, and re-layouts: 1.01 us -> 0.01 us
where the time goes in v2:
time: 78.7 us; the launch traced here: 78.1 us
  blocking collectives  37.2 us (47%)
  Pallas kernels  17.7 us (22%)
  waiting for transfers between devices  15.8 us (20%)
  starting transfers between devices  6.01 us (8%)
    all_to_all x1, blocking collectives, shards(): y = lax.all_to_all(y, 'ctx', split_axis=0, concat_axis=0, tiled=True)  22 us
    all_to_all x1, waiting for transfers between devices, shards(): lax.all_to_all(gated, 'ctx', split_axis=0, concat_axis=0, tiled=True)  15.8 us
    all_to_all x1, blocking collectives, shards(): peaks = lax.all_to_all(peaks, 'ch', split_axis=0, concat_axis=0, tiled=True)  15.2 us
    all_to_all x1, starting transfers between devices, shards(): lax.all_to_all(gated, 'ctx', split_axis=0, concat_axis=0, tiled=True)  6.01 us
    pallas_call x1, Pallas kernels, shards(): pl.pallas_call(functools.partial(conv_kernel, width=width), in_specs=[res...  5.7 us
    pallas_call x1, Pallas kernels, shards(): pl.pallas_call(functools.partial(scale_kernel, block=block), grid=steps,...  4.27 us
    pallas_call x1, Pallas kernels, shards(): pl.pallas_call(functools.partial(gate_kernel, block=block), grid=steps, i...  4.13 us
    pallas_call x1, Pallas kernels, shards(): pl.pallas_call(functools.partial(peak_kernel, block=block), grid=steps, i...  3.63 us
  transfers between devices with their start and end apart: 1, of which 1 were waited for; matrix products, arithmetic and copies ran while one was open for 1% of the time, Pallas kernels for 0%

profile of v2, /device:TPU:0, one launch (start us, length us, event | category | flops | bytes accessed | tf_op | source)
XLA Modules:
  0.0 78.1 jit_solution(461336314893549994)
XLA Ops:
  0.6 0.0 copy-start
  0.6 4.1 %gate.1 = bf16[1024,512]{1,0:T(8,128)(2,1)} custom-call(s32[3,2,8]{2,1,0:T(2,128)} %bitcast.4, bf16[1024,256]{1,0:T(8,128)(2,1)} %q_ref.1, bf16[1024,256]{1,0:T(8,128)(2,1)} %k_ref.5, bf16[1024,256]{1,0:T(8,128)(2,1)} %v_ref.5, bf16[1024,256]{1,0:T(8,128)(2,1)} %g_ref.5), custom_call_target="tpu_custom_call" | custom-call | tf_op jit(solution)/shard_map/gate/pallas_call | solution.py:243
  4.8 6.0 %all-to-all-start = ((bf16[16,64,512]{2,1,0:T(8,128)(2,1)}), bf16[16,64,512]{2,1,0:T(8,128)(2,1)S(1)}, u32[]{:S(2)}, u32[]{:S(2)}) async-start(bf16[16,64,512]{2,1,0:T(8,128)(2,1)} %bitcast.3), calls=%async_computation | async-start | bytes 2097152 | tf_op jit(solution)/shard_map/all_to_all | solution.py:251
  10.8 0.0 copy-done
  10.8 0.6 constant_dynamic-slice_fusion.taps_ref
  11.4 15.8 %all-to-all-done.x_ref = bf16[16,64,512]{2,1,0:T(8,128)(2,1)S(1)} async-done(((bf16[16,64,512]{2,1,0:T(8,128)(2,1)}), bf16[16,64,512]{2,1,0:T(8,128)(2,1)S(1)}, u32[]{:S(2)}, u32[]{:S(2)}) %all-to-all-start) | async-done | bytes 1048608 | tf_op jit(solution)/shard_map/all_to_all | solution.py:251
  27.3 5.7 %conv.1 = bf16[16,72,512]{2,1,0:T(8,128)(2,1)} custom-call(f32[4,1024]{1,0:T(4,128)} %constant_dynamic-slice_fusion.taps_ref, bf16[16,64,512]{2,1,0:T(8,128)(2,1)S(1)} %all-to-all-done.x_ref), custom_call_target="tpu_custom_call" | custom-call | tf_op jit(solution)/shard_map/conv/pallas_call | solution.py:265
  33.0 22.0 %all_to_all.19.y_ref = bf16[16,72,512]{2,1,0:T(8,128)(2,1)} all-to-all(bf16[16,72,512]{2,1,0:T(8,128)(2,1)} %conv.1), channel_id=1, replica_groups=mesh['ctx'=16,'ch'=8] {'ctx'}, dimensions={0} | all-to-all | bytes 2359296 | tf_op jit(solution)/shard_map/all_to_all | solution.py:274
  55.0 3.6 %peak.1 = f32[8,8,128]{2,1,0:T(8,128)} custom-call(s32[3,2,8]{2,1,0:T(2,128)} %bitcast.5, bf16[1024,256]{1,0:T(8,128)(2,1)} %k_ref.5, bf16[1024,256]{1,0:T(8,128)(2,1)} %v_ref.5, bf16[1024,256]{1,0:T(8,128)(2,1)} %g_ref.5, bf16[16,72,512]{2,1,0:T(8,128)(2,1)} %all_to_all.19.y_ref), custom_call_target="tpu_custom_call" | custom-call | tf_op jit(solution)/shard_map/peak/pallas_call | solution.py:277
  58.6 15.2 %all_to_all.20.peaks_ref = f32[8,8,128]{2,1,0:T(8,128)} all-to-all(f32[8,8,128]{2,1,0:T(8,128)} %peak.1), channel_id=1, replica_groups=mesh['ctx'=16,'ch'=8] {'ch'}, dimensions={0} | all-to-all | bytes 65536 | tf_op jit(solution)/shard_map/all_to_all | solution.py:286
  73.8 4.3 %scale.1 = (bf16[1024,256]{1,0:T(8,128)(2,1)}, bf16[1024,256]{1,0:T(8,128)(2,1)}, bf16[1024,256]{1,0:T(8,128)(2,1)}, f32[64,64]{1,0:T(8,128)}, f32[2,3]{1,0:T(2,128)}) custom-call(s32[3,2,8]{2,1,0:T(2,128)} %bitcast.6, bf16[1024,256]{1,0:T(8,128)(2,1)} %k_ref.5, bf16[1024,256]{1,0:T(8,128)(2,1)} %v_ref.5, bf16[1024,256]{1,0:T(8,128)(2,1)} %g_ref.5, ...), custom_call_target="tpu_custom_call" | custom-call | tf_op jit(solution)/shard_map/scale/pallas_call | solution.py:288
Async XLA Ops:
  0.6 10.2 %copy-start = (f32[64,1024]{1,0:T(8,128)S(1)}, f32[64,1024]{1,0:T(8,128)}, u32[]{:S(2)}) copy-start(f32[64,1024]{1,0:T(8,128)} %param.11) | copy-start | bytes 786436
  4.8 22.5 %all-to-all-start = ((bf16[16,64,512]{2,1,0:T(8,128)(2,1)}), bf16[16,64,512]{2,1,0:T(8,128)(2,1)S(1)}, u32[]{:S(2)}, u32[]{:S(2)}) async-start(bf16[16,64,512]{2,1,0:T(8,128)(2,1)} %bitcast.3), calls=%async_computation | async-start | bytes 2097152 | tf_op jit(solution)/shard_map/all_to_all | solution.py:251

commit v3 on v2

--- a/solution.py
+++ b/solution.py
@@ -166,7 +166,6 @@
 
 
 def gradients(e_ref, k_ref, v_ref, g_ref, y_ref, block):
-    first = pl.program_id(0) * (k_ref.shape[0] // block)
     part = y_ref.shape[1] - EXTRA
     each = block // part
     flip = mirror()
@@ -178,31 +177,29 @@
             [y_ref[s, :part, o * TILE : (o + 1) * TILE] for s in senders], axis=0
         )
         gz = jnp.dot(back, flip, preferred_element_type=jnp.float32)
-        v_real = v_ref[at, lanes].astype(jnp.float32) * power(e_ref, 2, first + n, p)
-        k_real = k_ref[at, lanes].astype(jnp.float32) * power(e_ref, 1, first + n, p)
+        v_real = v_ref[at, lanes].astype(jnp.float32) * power(e_ref, 2, n, p)
+        k_real = k_ref[at, lanes].astype(jnp.float32) * power(e_ref, 1, n, p)
         g = g_ref[at, lanes].astype(jnp.float32)
         yield p, at, lanes, (g * w, gz * v_real, gz * k_real)
 
 
-def peak_kernel(e_ref, k_ref, v_ref, g_ref, y_ref, out_ref, peak_ref, *, block):
-    @pl.when(pl.program_id(0) == 0)
-    def _():
-        peak_ref[...] = jnp.zeros(peak_ref.shape, jnp.float32)
-
+def peak_kernel(e_ref, k_ref, v_ref, g_ref, y_ref, out_ref, *, block):
+    tops = {}
     for p, at, lanes, products in gradients(e_ref, k_ref, v_ref, g_ref, y_ref, block):
         for i, product in enumerate(products):
-            top = jnp.max(jnp.abs(product), axis=0, keepdims=True)
-            spot = slice(p * 4 + i, p * 4 + i + 1)
-            peak_ref[spot, :] = jnp.maximum(peak_ref[spot, :], top)
-
-    @pl.when(pl.program_id(0) == pl.num_programs(0) - 1)
-    def _():
-        for n in range(out_ref.shape[0]):
-            out_ref[n] = peak_ref[...]
-
-
-def scale_kernel(e_ref, k_ref, v_ref, g_ref, y_ref, peaks_ref, oq_ref, ok_ref, ov_ref, lag_ref, top_ref, *, block):
-    top = jnp.max(peaks_ref[...], axis=0)
+            size = jnp.abs(product).reshape(block // 8, 8, TILE)
+            top = jnp.max(size, axis=0)
+            tops[p, i] = jnp.maximum(tops[p, i], top) if (p, i) in tops else top
+    blank = jnp.zeros((1, TILE), jnp.float32)
+    rows = []
+    for p in range(PARTS):
+        rows += [jnp.max(tops[p, i], axis=0, keepdims=True) for i in range(3)] + [blank]
+    best = jnp.concatenate(rows, axis=0)
+    out_ref[...] = best
+
+
+def scale_kernel(e_ref, k_ref, v_ref, g_ref, y_ref, peaks_ref, other_ref, oq_ref, ok_ref, ov_ref, lag_ref, top_ref, *, block):
+    top = jnp.maximum(peaks_ref[...], other_ref[...])
     for p in range(PARTS):
         for i in range(3):
             best = jnp.max(top[p * 4 + i : p * 4 + i + 1, :], axis=1, keepdims=True)
@@ -220,6 +217,18 @@
     for p, at, lanes, products in gradients(e_ref, k_ref, v_ref, g_ref, y_ref, block):
         for i, (product, ref) in enumerate(zip(products, (oq_ref, ok_ref, ov_ref))):
             ref[at, lanes] = (product * inverse[p * 4 + i : p * 4 + i + 1, :]).astype(jnp.bfloat16)
+
+
+def partners(devices):
+    rounds = []
+    size = 2
+    while size <= devices:
+        if size == 4:
+            rounds.append([i - i % 4 + 3 - i % 4 for i in range(devices)])
+        else:
+            rounds.append([i ^ (size // 2) for i in range(devices)])
+        size *= 2
+    return rounds
 
 
 def shards(q_vals, k_vals, v_vals, grad_out, exponents, filter_taps):
@@ -272,35 +281,30 @@
     )(own_taps, pltpu.with_memory_space_constraint(swapped.reshape(ctx, part, 2 * rows), pltpu.VMEM))
 
     y = lax.all_to_all(y, "ctx", split_axis=0, concat_axis=0, tiled=True)
-    mixed = pl.BlockSpec((tall // part, part + EXTRA, 2 * rows), lambda b: (b, 0, 0))
-    every = pl.BlockSpec((ch, 8, TILE), lambda b: (0, 0, 0))
+    near = lambda value: pltpu.with_memory_space_constraint(value, pltpu.VMEM)
+    held = (exponents, near(k_vals), near(v_vals), near(grad_out), near(y))
     peaks = pl.pallas_call(
         functools.partial(peak_kernel, block=block),
-        grid=steps,
-        in_specs=[scalars] + [tile] * 3 + [mixed],
-        out_specs=every,
-        out_shape=jax.ShapeDtypeStruct((ch, 8, TILE), jnp.float32),
-        scratch_shapes=[pltpu.VMEM((8, TILE), jnp.float32)],
+        in_specs=[resident] * 5,
+        out_specs=resident,
+        out_shape=jax.ShapeDtypeStruct((8, TILE), jnp.float32),
         name="peak",
-    )(exponents, k_vals, v_vals, grad_out, y)
-    peaks = lax.all_to_all(peaks, "ch", split_axis=0, concat_axis=0, tiled=True)
+    )(*held)
+    for partner in partners(ch)[:-1]:
+        peaks = jnp.maximum(peaks, lax.ppermute(peaks, "ch", list(enumerate(partner))))
+    others = lax.ppermute(peaks, "ch", list(enumerate(partners(ch)[-1])))
 
     oq, ok, ov, grad_filter, top = pl.pallas_call(
         functools.partial(scale_kernel, block=block),
-        grid=steps,
-        in_specs=[scalars] + [tile] * 3 + [mixed, every],
-        out_specs=[tile] * 3
-        + [
-            pl.BlockSpec((groups // steps[0], taps // ctx), lambda b: (b, 0)),
-            pl.BlockSpec((PARTS, 3), lambda b: (0, 0)),
-        ],
+        in_specs=[resident] * 7,
+        out_specs=[resident] * 5,
         out_shape=[jax.ShapeDtypeStruct((channels, rows), bf16)] * 3
         + [
             jax.ShapeDtypeStruct((groups, taps // ctx), jnp.float32),
             jax.ShapeDtypeStruct((PARTS, 3), jnp.float32),
         ],
         name="scale",
-    )(exponents, k_vals, v_vals, grad_out, y, peaks)
+    )(*held, near(peaks), near(others))
     return oq, ok, ov, grad_filter, top.T
 
 

time: 78.7 us -> 73.6 us (0.935)
  blocking collectives: 37.2 us -> 21.4 us
  starting transfers between devices: 6.01 us -> 13.8 us
  waiting for transfers between devices: 15.8 us -> 21.8 us
  Pallas kernels: 17.7 us -> 14 us
    all_to_all x1 -> x0, blocking collectives: 15.2 us -> none  [shards(): peaks = lax.all_to_all(peaks, 'ch', split_axis=0, concat_axis=0, tiled=True)]
    ppermute x0 -> x3, starting transfers between devices: none -> 7.8 us  [the longest x2 4.23 us: shards(): lax.ppermute(peaks, 'ch', list(enumerate(partner)))]
    ppermute x0 -> x3, waiting for transfers between devices: none -> 5.99 us  [the longest x2 4.41 us: shards(): lax.ppermute(peaks, 'ch', list(enumerate(partner)))]
    pallas_call x2, Pallas kernels: 7.9 us -> 4.2 us  [the longest x1 2.34 us: shards(): pl.pallas_call(functools.partial(scale_kernel, block=block), in_specs=[re...]
  transfers between devices with their start and end apart: 1 -> 4, of which waited for: 1 -> 4; matrix products, arithmetic and copies ran while one was open for 1% -> 1% of each run, Pallas kernels for 0% -> 0%
where the time goes in v3:
time: 73.6 us; the launch traced here: 73.1 us
  waiting for transfers between devices  21.8 us (30%)
  blocking collectives  21.4 us (29%)
  Pallas kernels  14 us (19%)
  starting transfers between devices  13.8 us (19%)
    all_to_all x1, blocking collectives, shards(): y = lax.all_to_all(y, 'ctx', split_axis=0, concat_axis=0, tiled=True)  21.4 us
    all_to_all x1, waiting for transfers between devices, shards(): lax.all_to_all(gated, 'ctx', split_axis=0, concat_axis=0, tiled=True)  15.8 us
    all_to_all x1, starting transfers between devices, shards(): lax.all_to_all(gated, 'ctx', split_axis=0, concat_axis=0, tiled=True)  6.01 us
    pallas_call x1, Pallas kernels, shards(): pl.pallas_call(functools.partial(conv_kernel, width=width), in_specs=[res...  5.7 us
    ppermute x2, waiting for transfers between devices, shards(): lax.ppermute(peaks, 'ch', list(enumerate(partner)))  4.41 us
    ppermute x2, starting transfers between devices, shards(): lax.ppermute(peaks, 'ch', list(enumerate(partner)))  4.23 us
    pallas_call x1, Pallas kernels, shards(): pl.pallas_call(functools.partial(gate_kernel, block=block), grid=steps, i...  4.13 us
    ppermute x1, starting transfers between devices, shards(): others = lax.ppermute(peaks, 'ch', list(enumerate(partners(ch)[-1])))  3.57 us
  transfers between devices with their start and end apart: 4, of which 4 were waited for; matrix products, arithmetic and copies ran while one was open for 1% of the time, Pallas kernels for 0%

profile of v3, /device:TPU:0, one launch (start us, length us, event | category | flops | bytes accessed | tf_op | source)
XLA Modules:
  0.0 73.1 jit_solution(16528511125985797806)
XLA Ops:
  0.6 0.0 copy-start
  0.6 4.1 %gate.1 = bf16[1024,512]{1,0:T(8,128)(2,1)} custom-call(s32[3,2,8]{2,1,0:T(2,128)} %bitcast.4, bf16[1024,256]{1,0:T(8,128)(2,1)} %q_ref.1, bf16[1024,256]{1,0:T(8,128)(2,1)} %k_ref.5, bf16[1024,256]{1,0:T(8,128)(2,1)} %v_ref.5, bf16[1024,256]{1,0:T(8,128)(2,1)} %g_ref.5), custom_call_target="tpu_custom_call" | custom-call | tf_op jit(solution)/shard_map/gate/pallas_call | solution.py:252
  4.8 6.0 %all-to-all-start = ((bf16[16,64,512]{2,1,0:T(8,128)(2,1)}), bf16[16,64,512]{2,1,0:T(8,128)(2,1)S(1)}, u32[]{:S(2)}, u32[]{:S(2)}) async-start(bf16[16,64,512]{2,1,0:T(8,128)(2,1)} %bitcast.3), calls=%async_computation | async-start | bytes 2097152 | tf_op jit(solution)/shard_map/all_to_all | solution.py:260
  10.8 0.0 copy-done
  10.8 0.6 constant_dynamic-slice_fusion.taps_ref
  11.4 15.8 %all-to-all-done.x_ref = bf16[16,64,512]{2,1,0:T(8,128)(2,1)S(1)} async-done(((bf16[16,64,512]{2,1,0:T(8,128)(2,1)}), bf16[16,64,512]{2,1,0:T(8,128)(2,1)S(1)}, u32[]{:S(2)}, u32[]{:S(2)}) %all-to-all-start) | async-done | bytes 1048608 | tf_op jit(solution)/shard_map/all_to_all | solution.py:260
  27.3 5.7 %conv.1 = bf16[16,72,512]{2,1,0:T(8,128)(2,1)} custom-call(f32[4,1024]{1,0:T(4,128)} %constant_dynamic-slice_fusion.taps_ref, bf16[16,64,512]{2,1,0:T(8,128)(2,1)S(1)} %all-to-all-done.x_ref), custom_call_target="tpu_custom_call" | custom-call | tf_op jit(solution)/shard_map/conv/pallas_call | solution.py:274
  33.0 0.0 copy-start.1
  33.0 0.0 copy-start.2
  33.0 0.0 copy-start.3
  33.0 21.4 %all_to_all.14.y_ref = bf16[16,72,512]{2,1,0:T(8,128)(2,1)S(1)} all-to-all(bf16[16,72,512]{2,1,0:T(8,128)(2,1)} %conv.1), channel_id=1, replica_groups=mesh['ctx'=16,'ch'=8] {'ctx'}, dimensions={0} | all-to-all | bytes 2359296 | tf_op jit(solution)/shard_map/all_to_all | solution.py:283
  54.4 0.0 copy-done.1
  54.4 0.0 copy-done.2
  54.4 0.0 copy-done.3
  54.4 1.9 %peak.1 = f32[8,128]{1,0:T(8,128)} custom-call(s32[3,2,8]{2,1,0:T(2,128)} %bitcast.5, bf16[1024,256]{1,0:T(8,128)(2,1)S(1)} %copy-done.1, bf16[1024,256]{1,0:T(8,128)(2,1)S(1)} %copy-done.2, bf16[1024,256]{1,0:T(8,128)(2,1)S(1)} %copy-done.3, bf16[16,72,512]{2,1,0:T(8,128)(2,1)S(1)} %all_to_all.14.y_ref), custom_call_target="tpu_custom_call" | custom-call | tf_op jit(solution)/shard_map/peak/pallas_call | solution.py:286
  56.3 1.5 %collective-permute-start = (f32[8,128]{1,0:T(8,128)}, f32[8,128]{1,0:T(8,128)S(1)}, u32[]{:S(2)}, u32[]{:S(2)}) collective-permute-start(f32[8,128]{1,0:T(8,128)} %peak.1), channel_id=1, source_target_pairs={{0,1},{1,0},{2,3},{3,2},{4,5},{5,4},{6,7},{7,6},{8,9},{9,8},{10,11... | collective-permute-start | bytes 12296 | tf_op jit(solution)/shard_map/ppermute | solution.py:294
  57.8 2.3 %collective-permute-done = f32[8,128]{1,0:T(8,128)S(1)} collective-permute-done((f32[8,128]{1,0:T(8,128)}, f32[8,128]{1,0:T(8,128)S(1)}, u32[]{:S(2)}, u32[]{:S(2)}) %collective-permute-start) | collective-permute-done | bytes 4128 | tf_op jit(solution)/shard_map/ppermute | solution.py:294
  60.1 0.7 max.6
  60.8 2.7 %collective-permute-start.1 = (f32[8,128]{1,0:T(8,128)S(1)}, f32[8,128]{1,0:T(8,128)S(1)}, u32[]{:S(2)}, u32[]{:S(2)}) collective-permute-start(f32[8,128]{1,0:T(8,128)S(1)} %max.6), channel_id=1, source_target_pairs={{0,3},{1,2},{2,1},{3,0},{4,7},{5,6},{6,5},{7,4},{8,11},{9,10},{10,... | collective-permute-start | bytes 12296 | tf_op jit(solution)/shard_map/ppermute | solution.py:294
  63.6 2.1 %collective-permute-done.1 = f32[8,128]{1,0:T(8,128)S(1)} collective-permute-done((f32[8,128]{1,0:T(8,128)S(1)}, f32[8,128]{1,0:T(8,128)S(1)}, u32[]{:S(2)}, u32[]{:S(2)}) %collective-permute-start.1) | collective-permute-done | bytes 4128 | tf_op jit(solution)/shard_map/ppermute | solution.py:294
  65.6 3.6 %collective-permute-start.2 = (f32[8,128]{1,0:T(8,128)S(1)}, f32[8,128]{1,0:T(8,128)S(1)}, u32[]{:S(2)}, u32[]{:S(2)}) collective-permute-start(f32[8,128]{1,0:T(8,128)S(1)} %max.7.peaks_ref), channel_id=1, source_target_pairs={{0,4},{1,5},{2,6},{3,7},{4,0},{5,1},{6,2},{7,3},{8,12},{9,13},{10,... | collective-permute-start | bytes 12296 | tf_op jit(solution)/shard_map/ppermute | solution.py:295
  69.2 1.6 %collective-permute-done.2.other_ref = f32[8,128]{1,0:T(8,128)S(1)} collective-permute-done((f32[8,128]{1,0:T(8,128)S(1)}, f32[8,128]{1,0:T(8,128)S(1)}, u32[]{:S(2)}, u32[]{:S(2)}) %collective-permute-start.2) | collective-permute-done | bytes 4128 | tf_op jit(solution)/shard_map/ppermute | solution.py:295
  70.8 2.3 %scale.1 = (bf16[1024,256]{1,0:T(8,128)(2,1)}, bf16[1024,256]{1,0:T(8,128)(2,1)}, bf16[1024,256]{1,0:T(8,128)(2,1)}, f32[64,64]{1,0:T(8,128)}, f32[2,3]{1,0:T(2,128)}) custom-call(s32[3,2,8]{2,1,0:T(2,128)} %bitcast.6, bf16[1024,256]{1,0:T(8,128)(2,1)S(1)} %copy-done.1, bf16[1024,256]{1,0:T(8,128)(2,1)S(1)} %copy-done.2, bf16[1024,256]{1,0:T(8,128)(2,1)S(1)} %copy-done.3, ...), custom_call_target="tpu_custom_call" | custom-call | tf_op jit(solution)/shard_map/scale/pallas_call | solution.py:297
  (1 shorter events, 0.0 us)
Async XLA Ops:
  0.6 10.2 %copy-start = (f32[64,1024]{1,0:T(8,128)S(1)}, f32[64,1024]{1,0:T(8,128)}, u32[]{:S(2)}) copy-start(f32[64,1024]{1,0:T(8,128)} %param.11) | copy-start | bytes 786436
  4.8 22.5 %all-to-all-start = ((bf16[16,64,512]{2,1,0:T(8,128)(2,1)}), bf16[16,64,512]{2,1,0:T(8,128)(2,1)S(1)}, u32[]{:S(2)}, u32[]{:S(2)}) async-start(bf16[16,64,512]{2,1,0:T(8,128)(2,1)} %bitcast.3), calls=%async_computation | async-start | bytes 2097152 | tf_op jit(solution)/shard_map/all_to_all | solution.py:260
  33.0 21.4 %copy-start.1 = (bf16[1024,256]{1,0:T(8,128)(2,1)S(1)}, bf16[1024,256]{1,0:T(8,128)(2,1)}, u32[]{:S(2)}) copy-start(bf16[1024,256]{1,0:T(8,128)(2,1)} %k_ref.5) | copy-start | bytes 1572868
  33.0 21.4 %copy-start.2 = (bf16[1024,256]{1,0:T(8,128)(2,1)S(1)}, bf16[1024,256]{1,0:T(8,128)(2,1)}, u32[]{:S(2)}) copy-start(bf16[1024,256]{1,0:T(8,128)(2,1)} %v_ref.5) | copy-start | bytes 1572868
  33.0 21.4 %copy-start.3 = (bf16[1024,256]{1,0:T(8,128)(2,1)S(1)}, bf16[1024,256]{1,0:T(8,128)(2,1)}, u32[]{:S(2)}) copy-start(bf16[1024,256]{1,0:T(8,128)(2,1)} %g_ref.5) | copy-start | bytes 1572868
  56.3 3.8 %collective-permute-start = (f32[8,128]{1,0:T(8,128)}, f32[8,128]{1,0:T(8,128)S(1)}, u32[]{:S(2)}, u32[]{:S(2)}) collective-permute-start(f32[8,128]{1,0:T(8,128)} %peak.1), channel_id=1, source_target_pairs={{0,1},{1,0},{2,3},{3,2},{4,5},{5,4},{6,7},{7,6},{8,9},{9,8},{10,11... | collective-permute-start | bytes 12296 | tf_op jit(solution)/shard_map/ppermute | solution.py:294
  60.8 4.8 %collective-permute-start.1 = (f32[8,128]{1,0:T(8,128)S(1)}, f32[8,128]{1,0:T(8,128)S(1)}, u32[]{:S(2)}, u32[]{:S(2)}) collective-permute-start(f32[8,128]{1,0:T(8,128)S(1)} %max.6), channel_id=1, source_target_pairs={{0,3},{1,2},{2,1},{3,0},{4,7},{5,6},{6,5},{7,4},{8,11},{9,10},{10,... | collective-permute-start | bytes 12296 | tf_op jit(solution)/shard_map/ppermute | solution.py:294
  65.6 5.2 %collective-permute-start.2 = (f32[8,128]{1,0:T(8,128)S(1)}, f32[8,128]{1,0:T(8,128)S(1)}, u32[]{:S(2)}, u32[]{:S(2)}) collective-permute-start(f32[8,128]{1,0:T(8,128)S(1)} %max.7.peaks_ref), channel_id=1, source_target_pairs={{0,4},{1,5},{2,6},{3,7},{4,0},{5,1},{6,2},{7,3},{8,12},{9,13},{10,... | collective-permute-start | bytes 12296 | tf_op jit(solution)/shard_map/ppermute | solution.py:295

commit v4 on v3

--- a/solution.py
+++ b/solution.py
@@ -241,7 +241,7 @@
     part = channels // ctx
     mine = groups // ctx
     span = taps + TILE
-    tall = 2 * block
+    tall = block
     steps = (channels // tall,)
     exponents = exponents.transpose(0, 2, 1)
     scalars = pl.BlockSpec(exponents.shape, lambda b: (0, 0, 0))
@@ -287,7 +287,7 @@
         functools.partial(peak_kernel, block=block),
         in_specs=[resident] * 5,
         out_specs=resident,
-        out_shape=jax.ShapeDtypeStruct((8, TILE), jnp.float32),
+        out_shape=pltpu.VMEM((8, TILE), jnp.float32),
         name="peak",
     )(*held)
     for partner in partners(ch)[:-1]:

time: 73.6 us -> 74.5 us (1.012)
  Pallas kernels: 14 us -> 15.5 us
    pallas_call x1, Pallas kernels: 4.13 us -> 6.23 us  [shards(): pl.pallas_call(functools.partial(gate_kernel, block=block), grid=steps, i...]
where the time goes in v4:
time: 74.5 us; the launch traced here: 73.8 us
  waiting for transfers between devices  21.6 us (29%)
  blocking collectives  21.4 us (29%)
  Pallas kernels  15.5 us (21%)
  starting transfers between devices  13.9 us (19%)
    all_to_all x1, blocking collectives, shards(): y = lax.all_to_all(y, 'ctx', split_axis=0, concat_axis=0, tiled=True)  21.4 us
    all_to_all x1, waiting for transfers between devices, shards(): lax.all_to_all(gated, 'ctx', split_axis=0, concat_axis=0, tiled=True)  15.8 us
    pallas_call x1, Pallas kernels, shards(): pl.pallas_call(functools.partial(gate_kernel, block=block), grid=steps, i...  6.23 us
    all_to_all x1, starting transfers between devices, shards(): lax.all_to_all(gated, 'ctx', split_axis=0, concat_axis=0, tiled=True)  6.01 us
    pallas_call x1, Pallas kernels, shards(): pl.pallas_call(functools.partial(conv_kernel, width=width), in_specs=[res...  5.69 us
    ppermute x2, starting transfers between devices, shards(): lax.ppermute(peaks, 'ch', list(enumerate(partner)))  4.33 us
    ppermute x2, waiting for transfers between devices, shards(): lax.ppermute(peaks, 'ch', list(enumerate(partner)))  4.18 us
    ppermute x1, starting transfers between devices, shards(): others = lax.ppermute(peaks, 'ch', list(enumerate(partners(ch)[-1])))  3.58 us
  transfers between devices with their start and end apart: 4, of which 4 were waited for; matrix products, arithmetic and copies ran while one was open for 1% of the time, Pallas kernels for 0%

profile of v4, /device:TPU:0, one launch (start us, length us, event | category | flops | bytes accessed | tf_op | source)
XLA Modules:
  0.0 73.8 jit_solution(5477430473907991089)
XLA Ops:
  0.6 0.0 copy-start
  0.6 6.2 %gate.1 = bf16[1024,512]{1,0:T(8,128)(2,1)} custom-call(s32[3,2,8]{2,1,0:T(2,128)} %bitcast.4, bf16[1024,256]{1,0:T(8,128)(2,1)} %q_ref.1, bf16[1024,256]{1,0:T(8,128)(2,1)} %k_ref.5, bf16[1024,256]{1,0:T(8,128)(2,1)} %v_ref.5, bf16[1024,256]{1,0:T(8,128)(2,1)} %g_ref.5), custom_call_target="tpu_custom_call" | custom-call | tf_op jit(solution)/shard_map/gate/pallas_call | solution.py:252
  6.9 6.0 %all-to-all-start = ((bf16[16,64,512]{2,1,0:T(8,128)(2,1)}), bf16[16,64,512]{2,1,0:T(8,128)(2,1)S(1)}, u32[]{:S(2)}, u32[]{:S(2)}) async-start(bf16[16,64,512]{2,1,0:T(8,128)(2,1)} %bitcast.3), calls=%async_computation | async-start | bytes 2097152 | tf_op jit(solution)/shard_map/all_to_all | solution.py:260
  12.9 0.0 copy-done
  12.9 0.6 constant_dynamic-slice_fusion.taps_ref
  13.5 15.8 %all-to-all-done.x_ref = bf16[16,64,512]{2,1,0:T(8,128)(2,1)S(1)} async-done(((bf16[16,64,512]{2,1,0:T(8,128)(2,1)}), bf16[16,64,512]{2,1,0:T(8,128)(2,1)S(1)}, u32[]{:S(2)}, u32[]{:S(2)}) %all-to-all-start) | async-done | bytes 1048608 | tf_op jit(solution)/shard_map/all_to_all | solution.py:260
  29.4 5.7 %conv.1 = bf16[16,72,512]{2,1,0:T(8,128)(2,1)} custom-call(f32[4,1024]{1,0:T(4,128)} %constant_dynamic-slice_fusion.taps_ref, bf16[16,64,512]{2,1,0:T(8,128)(2,1)S(1)} %all-to-all-done.x_ref), custom_call_target="tpu_custom_call" | custom-call | tf_op jit(solution)/shard_map/conv/pallas_call | solution.py:274
  35.1 0.0 copy-start.1
  35.1 0.0 copy-start.2
  35.1 0.0 copy-start.3
  35.1 21.4 %all_to_all.14.y_ref = bf16[16,72,512]{2,1,0:T(8,128)(2,1)S(1)} all-to-all(bf16[16,72,512]{2,1,0:T(8,128)(2,1)} %conv.1), channel_id=1, replica_groups=mesh['ctx'=16,'ch'=8] {'ctx'}, dimensions={0} | all-to-all | bytes 2359296 | tf_op jit(solution)/shard_map/all_to_all | solution.py:283
  56.5 0.0 copy-done.1
  56.5 0.0 copy-done.2
  56.5 0.0 copy-done.3
  56.5 1.3 %peak.1 = f32[8,128]{1,0:T(8,128)S(1)} custom-call(s32[3,2,8]{2,1,0:T(2,128)} %bitcast.5, bf16[1024,256]{1,0:T(8,128)(2,1)S(1)} %copy-done.1, bf16[1024,256]{1,0:T(8,128)(2,1)S(1)} %copy-done.2, bf16[1024,256]{1,0:T(8,128)(2,1)S(1)} %copy-done.3, bf16[16,72,512]{2,1,0:T(8,128)(2,1)S(1)} %all_to_all.14.y_ref), custom_call_target="tpu_custom_call" | custom-call | tf_op jit(solution)/shard_map/peak/pallas_call | solution.py:286
  57.8 1.6 %collective-permute-start = (f32[8,128]{1,0:T(8,128)S(1)}, f32[8,128]{1,0:T(8,128)S(1)}, u32[]{:S(2)}, u32[]{:S(2)}) collective-permute-start(f32[8,128]{1,0:T(8,128)S(1)} %peak.1), channel_id=1, source_target_pairs={{0,1},{1,0},{2,3},{3,2},{4,5},{5,4},{6,7},{7,6},{8,9},{9,8},{10,11... | collective-permute-start | bytes 12296 | tf_op jit(solution)/shard_map/ppermute | solution.py:294
  59.4 2.1 %collective-permute-done = f32[8,128]{1,0:T(8,128)S(1)} collective-permute-done((f32[8,128]{1,0:T(8,128)S(1)}, f32[8,128]{1,0:T(8,128)S(1)}, u32[]{:S(2)}, u32[]{:S(2)}) %collective-permute-start) | collective-permute-done | bytes 4128 | tf_op jit(solution)/shard_map/ppermute | solution.py:294
  61.5 2.8 %collective-permute-start.1 = (f32[8,128]{1,0:T(8,128)S(1)}, f32[8,128]{1,0:T(8,128)S(1)}, u32[]{:S(2)}, u32[]{:S(2)}) collective-permute-start(f32[8,128]{1,0:T(8,128)S(1)} %max.6), channel_id=1, source_target_pairs={{0,3},{1,2},{2,1},{3,0},{4,7},{5,6},{6,5},{7,4},{8,11},{9,10},{10,... | collective-permute-start | bytes 12296 | tf_op jit(solution)/shard_map/ppermute | solution.py:294
  64.2 2.1 %collective-permute-done.1 = f32[8,128]{1,0:T(8,128)S(1)} collective-permute-done((f32[8,128]{1,0:T(8,128)S(1)}, f32[8,128]{1,0:T(8,128)S(1)}, u32[]{:S(2)}, u32[]{:S(2)}) %collective-permute-start.1) | collective-permute-done | bytes 4128 | tf_op jit(solution)/shard_map/ppermute | solution.py:294
  66.3 3.6 %collective-permute-start.2 = (f32[8,128]{1,0:T(8,128)S(1)}, f32[8,128]{1,0:T(8,128)S(1)}, u32[]{:S(2)}, u32[]{:S(2)}) collective-permute-start(f32[8,128]{1,0:T(8,128)S(1)} %max.7.peaks_ref), channel_id=1, source_target_pairs={{0,4},{1,5},{2,6},{3,7},{4,0},{5,1},{6,2},{7,3},{8,12},{9,13},{10,... | collective-permute-start | bytes 12296 | tf_op jit(solution)/shard_map/ppermute | solution.py:295
  69.9 1.6 %collective-permute-done.2.other_ref = f32[8,128]{1,0:T(8,128)S(1)} collective-permute-done((f32[8,128]{1,0:T(8,128)S(1)}, f32[8,128]{1,0:T(8,128)S(1)}, u32[]{:S(2)}, u32[]{:S(2)}) %collective-permute-start.2) | collective-permute-done | bytes 4128 | tf_op jit(solution)/shard_map/ppermute | solution.py:295
  71.5 2.3 %scale.1 = (bf16[1024,256]{1,0:T(8,128)(2,1)}, bf16[1024,256]{1,0:T(8,128)(2,1)}, bf16[1024,256]{1,0:T(8,128)(2,1)}, f32[64,64]{1,0:T(8,128)}, f32[2,3]{1,0:T(2,128)}) custom-call(s32[3,2,8]{2,1,0:T(2,128)} %bitcast.6, bf16[1024,256]{1,0:T(8,128)(2,1)S(1)} %copy-done.1, bf16[1024,256]{1,0:T(8,128)(2,1)S(1)} %copy-done.2, bf16[1024,256]{1,0:T(8,128)(2,1)S(1)} %copy-done.3, ...), custom_call_target="tpu_custom_call" | custom-call | tf_op jit(solution)/shard_map/scale/pallas_call | solution.py:297
  (2 shorter events, 0.0 us)
Async XLA Ops:
  0.6 12.3 %copy-start = (f32[64,1024]{1,0:T(8,128)S(1)}, f32[64,1024]{1,0:T(8,128)}, u32[]{:S(2)}) copy-start(f32[64,1024]{1,0:T(8,128)} %param.11) | copy-start | bytes 786436
  6.9 22.5 %all-to-all-start = ((bf16[16,64,512]{2,1,0:T(8,128)(2,1)}), bf16[16,64,512]{2,1,0:T(8,128)(2,1)S(1)}, u32[]{:S(2)}, u32[]{:S(2)}) async-start(bf16[16,64,512]{2,1,0:T(8,128)(2,1)} %bitcast.3), calls=%async_computation | async-start | bytes 2097152 | tf_op jit(solution)/shard_map/all_to_all | solution.py:260
  35.1 21.4 %copy-start.1 = (bf16[1024,256]{1,0:T(8,128)(2,1)S(1)}, bf16[1024,256]{1,0:T(8,128)(2,1)}, u32[]{:S(2)}) copy-start(bf16[1024,256]{1,0:T(8,128)(2,1)} %k_ref.5) | copy-start | bytes 1572868
  35.1 21.4 %copy-start.2 = (bf16[1024,256]{1,0:T(8,128)(2,1)S(1)}, bf16[1024,256]{1,0:T(8,128)(2,1)}, u32[]{:S(2)}) copy-start(bf16[1024,256]{1,0:T(8,128)(2,1)} %v_ref.5) | copy-start | bytes 1572868
  35.1 21.4 %copy-start.3 = (bf16[1024,256]{1,0:T(8,128)(2,1)S(1)}, bf16[1024,256]{1,0:T(8,128)(2,1)}, u32[]{:S(2)}) copy-start(bf16[1024,256]{1,0:T(8,128)(2,1)} %g_ref.5) | copy-start | bytes 1572868
  57.8 3.7 %collective-permute-start = (f32[8,128]{1,0:T(8,128)S(1)}, f32[8,128]{1,0:T(8,128)S(1)}, u32[]{:S(2)}, u32[]{:S(2)}) collective-permute-start(f32[8,128]{1,0:T(8,128)S(1)} %peak.1), channel_id=1, source_target_pairs={{0,1},{1,0},{2,3},{3,2},{4,5},{5,4},{6,7},{7,6},{8,9},{9,8},{10,11... | collective-permute-start | bytes 12296 | tf_op jit(solution)/shard_map/ppermute | solution.py:294
  61.5 4.8 %collective-permute-start.1 = (f32[8,128]{1,0:T(8,128)S(1)}, f32[8,128]{1,0:T(8,128)S(1)}, u32[]{:S(2)}, u32[]{:S(2)}) collective-permute-start(f32[8,128]{1,0:T(8,128)S(1)} %max.6), channel_id=1, source_target_pairs={{0,3},{1,2},{2,1},{3,0},{4,7},{5,6},{6,5},{7,4},{8,11},{9,10},{10,... | collective-permute-start | bytes 12296 | tf_op jit(solution)/shard_map/ppermute | solution.py:294
  66.3 5.2 %collective-permute-start.2 = (f32[8,128]{1,0:T(8,128)S(1)}, f32[8,128]{1,0:T(8,128)S(1)}, u32[]{:S(2)}, u32[]{:S(2)}) collective-permute-start(f32[8,128]{1,0:T(8,128)S(1)} %max.7.peaks_ref), channel_id=1, source_target_pairs={{0,4},{1,5},{2,6},{3,7},{4,0},{5,1},{6,2},{7,3},{8,12},{9,13},{10,... | collective-permute-start | bytes 12296 | tf_op jit(solution)/shard_map/ppermute | solution.py:295

commit v5 on v4

--- a/solution.py
+++ b/solution.py
@@ -241,7 +241,7 @@
     part = channels // ctx
     mine = groups // ctx
     span = taps + TILE
-    tall = block
+    tall = 4 * block
     steps = (channels // tall,)
     exponents = exponents.transpose(0, 2, 1)
     scalars = pl.BlockSpec(exponents.shape, lambda b: (0, 0, 0))

time: 74.5 us -> 70.8 us (0.950)
  Pallas kernels: 15.5 us -> 12.1 us
    pallas_call x1, Pallas kernels: 6.23 us -> 2.82 us  [shards(): pl.pallas_call(functools.partial(gate_kernel, block=block), grid=steps, i...]
where the time goes in v5:
time: 70.8 us; the launch traced here: 70.4 us
  waiting for transfers between devices  21.6 us (31%)
  blocking collectives  21.4 us (30%)
  starting transfers between devices  13.9 us (20%)
  Pallas kernels  12.1 us (17%)
    all_to_all x1, blocking collectives, shards(): y = lax.all_to_all(y, 'ctx', split_axis=0, concat_axis=0, tiled=True)  21.4 us
    all_to_all x1, waiting for transfers between devices, shards(): lax.all_to_all(gated, 'ctx', split_axis=0, concat_axis=0, tiled=True)  15.8 us
    all_to_all x1, starting transfers between devices, shards(): lax.all_to_all(gated, 'ctx', split_axis=0, concat_axis=0, tiled=True)  6.01 us
    pallas_call x1, Pallas kernels, shards(): pl.pallas_call(functools.partial(conv_kernel, width=width), in_specs=[res...  5.69 us
    ppermute x2, starting transfers between devices, shards(): lax.ppermute(peaks, 'ch', list(enumerate(partner)))  4.34 us
    ppermute x2, waiting for transfers between devices, shards(): lax.ppermute(peaks, 'ch', list(enumerate(partner)))  4.17 us
    ppermute x1, starting transfers between devices, shards(): others = lax.ppermute(peaks, 'ch', list(enumerate(partners(ch)[-1])))  3.58 us
    pallas_call x1, Pallas kernels, shards(): pl.pallas_call(functools.partial(gate_kernel, block=block), grid=steps, i...  2.82 us
  transfers between devices with their start and end apart: 4, of which 4 were waited for; matrix products, arithmetic and copies ran while one was open for 1% of the time, Pallas kernels for 0%

profile of v5, /device:TPU:0, one launch (start us, length us, event | category | flops | bytes accessed | tf_op | source)
XLA Modules:
  0.0 70.4 jit_solution(13166462046315184042)
XLA Ops:
  0.6 0.0 copy-start
  0.6 2.8 %gate.1 = bf16[1024,512]{1,0:T(8,128)(2,1)} custom-call(s32[3,2,8]{2,1,0:T(2,128)} %bitcast.4, bf16[1024,256]{1,0:T(8,128)(2,1)} %q_ref.1, bf16[1024,256]{1,0:T(8,128)(2,1)} %k_ref.5, bf16[1024,256]{1,0:T(8,128)(2,1)} %v_ref.5, bf16[1024,256]{1,0:T(8,128)(2,1)} %g_ref.5), custom_call_target="tpu_custom_call" | custom-call | tf_op jit(solution)/shard_map/gate/pallas_call | solution.py:252
  3.5 6.0 %all-to-all-start = ((bf16[16,64,512]{2,1,0:T(8,128)(2,1)}), bf16[16,64,512]{2,1,0:T(8,128)(2,1)S(1)}, u32[]{:S(2)}, u32[]{:S(2)}) async-start(bf16[16,64,512]{2,1,0:T(8,128)(2,1)} %bitcast.3), calls=%async_computation | async-start | bytes 2097152 | tf_op jit(solution)/shard_map/all_to_all | solution.py:260
  9.5 0.0 copy-done
  9.5 0.6 constant_dynamic-slice_fusion.taps_ref
  10.1 15.8 %all-to-all-done.x_ref = bf16[16,64,512]{2,1,0:T(8,128)(2,1)S(1)} async-done(((bf16[16,64,512]{2,1,0:T(8,128)(2,1)}), bf16[16,64,512]{2,1,0:T(8,128)(2,1)S(1)}, u32[]{:S(2)}, u32[]{:S(2)}) %all-to-all-start) | async-done | bytes 1048608 | tf_op jit(solution)/shard_map/all_to_all | solution.py:260
  26.0 5.7 %conv.1 = bf16[16,72,512]{2,1,0:T(8,128)(2,1)} custom-call(f32[4,1024]{1,0:T(4,128)} %constant_dynamic-slice_fusion.taps_ref, bf16[16,64,512]{2,1,0:T(8,128)(2,1)S(1)} %all-to-all-done.x_ref), custom_call_target="tpu_custom_call" | custom-call | tf_op jit(solution)/shard_map/conv/pallas_call | solution.py:274
  31.6 0.0 copy-start.1
  31.7 0.0 copy-start.2
  31.7 0.0 copy-start.3
  31.7 21.4 %all_to_all.14.y_ref = bf16[16,72,512]{2,1,0:T(8,128)(2,1)S(1)} all-to-all(bf16[16,72,512]{2,1,0:T(8,128)(2,1)} %conv.1), channel_id=1, replica_groups=mesh['ctx'=16,'ch'=8] {'ctx'}, dimensions={0} | all-to-all | bytes 2359296 | tf_op jit(solution)/shard_map/all_to_all | solution.py:283
  53.1 0.0 copy-done.1
  53.1 0.0 copy-done.2
  53.1 0.0 copy-done.3
  53.1 1.3 %peak.1 = f32[8,128]{1,0:T(8,128)S(1)} custom-call(s32[3,2,8]{2,1,0:T(2,128)} %bitcast.5, bf16[1024,256]{1,0:T(8,128)(2,1)S(1)} %copy-done.1, bf16[1024,256]{1,0:T(8,128)(2,1)S(1)} %copy-done.2, bf16[1024,256]{1,0:T(8,128)(2,1)S(1)} %copy-done.3, bf16[16,72,512]{2,1,0:T(8,128)(2,1)S(1)} %all_to_all.14.y_ref), custom_call_target="tpu_custom_call" | custom-call | tf_op jit(solution)/shard_map/peak/pallas_call | solution.py:286
  54.4 1.6 %collective-permute-start = (f32[8,128]{1,0:T(8,128)S(1)}, f32[8,128]{1,0:T(8,128)S(1)}, u32[]{:S(2)}, u32[]{:S(2)}) collective-permute-start(f32[8,128]{1,0:T(8,128)S(1)} %peak.1), channel_id=1, source_target_pairs={{0,1},{1,0},{2,3},{3,2},{4,5},{5,4},{6,7},{7,6},{8,9},{9,8},{10,11... | collective-permute-start | bytes 12296 | tf_op jit(solution)/shard_map/ppermute | solution.py:294
  55.9 2.1 %collective-permute-done = f32[8,128]{1,0:T(8,128)S(1)} collective-permute-done((f32[8,128]{1,0:T(8,128)S(1)}, f32[8,128]{1,0:T(8,128)S(1)}, u32[]{:S(2)}, u32[]{:S(2)}) %collective-permute-start) | collective-permute-done | bytes 4128 | tf_op jit(solution)/shard_map/ppermute | solution.py:294
  58.1 2.8 %collective-permute-start.1 = (f32[8,128]{1,0:T(8,128)S(1)}, f32[8,128]{1,0:T(8,128)S(1)}, u32[]{:S(2)}, u32[]{:S(2)}) collective-permute-start(f32[8,128]{1,0:T(8,128)S(1)} %max.6), channel_id=1, source_target_pairs={{0,3},{1,2},{2,1},{3,0},{4,7},{5,6},{6,5},{7,4},{8,11},{9,10},{10,... | collective-permute-start | bytes 12296 | tf_op jit(solution)/shard_map/ppermute | solution.py:294
  60.8 2.1 %collective-permute-done.1 = f32[8,128]{1,0:T(8,128)S(1)} collective-permute-done((f32[8,128]{1,0:T(8,128)S(1)}, f32[8,128]{1,0:T(8,128)S(1)}, u32[]{:S(2)}, u32[]{:S(2)}) %collective-permute-start.1) | collective-permute-done | bytes 4128 | tf_op jit(solution)/shard_map/ppermute | solution.py:294
  62.9 3.6 %collective-permute-start.2 = (f32[8,128]{1,0:T(8,128)S(1)}, f32[8,128]{1,0:T(8,128)S(1)}, u32[]{:S(2)}, u32[]{:S(2)}) collective-permute-start(f32[8,128]{1,0:T(8,128)S(1)} %max.7.peaks_ref), channel_id=1, source_target_pairs={{0,4},{1,5},{2,6},{3,7},{4,0},{5,1},{6,2},{7,3},{8,12},{9,13},{10,... | collective-permute-start | bytes 12296 | tf_op jit(solution)/shard_map/ppermute | solution.py:295
  66.5 1.6 %collective-permute-done.2.other_ref = f32[8,128]{1,0:T(8,128)S(1)} collective-permute-done((f32[8,128]{1,0:T(8,128)S(1)}, f32[8,128]{1,0:T(8,128)S(1)}, u32[]{:S(2)}, u32[]{:S(2)}) %collective-permute-start.2) | collective-permute-done | bytes 4128 | tf_op jit(solution)/shard_map/ppermute | solution.py:295
  68.1 2.3 %scale.1 = (bf16[1024,256]{1,0:T(8,128)(2,1)}, bf16[1024,256]{1,0:T(8,128)(2,1)}, bf16[1024,256]{1,0:T(8,128)(2,1)}, f32[64,64]{1,0:T(8,128)}, f32[2,3]{1,0:T(2,128)}) custom-call(s32[3,2,8]{2,1,0:T(2,128)} %bitcast.6, bf16[1024,256]{1,0:T(8,128)(2,1)S(1)} %copy-done.1, bf16[1024,256]{1,0:T(8,128)(2,1)S(1)} %copy-done.2, bf16[1024,256]{1,0:T(8,128)(2,1)S(1)} %copy-done.3, ...), custom_call_target="tpu_custom_call" | custom-call | tf_op jit(solution)/shard_map/scale/pallas_call | solution.py:297
  (2 shorter events, 0.0 us)
Async XLA Ops:
  0.6 8.9 %copy-start = (f32[64,1024]{1,0:T(8,128)S(1)}, f32[64,1024]{1,0:T(8,128)}, u32[]{:S(2)}) copy-start(f32[64,1024]{1,0:T(8,128)} %param.11) | copy-start | bytes 786436
  3.5 22.5 %all-to-all-start = ((bf16[16,64,512]{2,1,0:T(8,128)(2,1)}), bf16[16,64,512]{2,1,0:T(8,128)(2,1)S(1)}, u32[]{:S(2)}, u32[]{:S(2)}) async-start(bf16[16,64,512]{2,1,0:T(8,128)(2,1)} %bitcast.3), calls=%async_computation | async-start | bytes 2097152 | tf_op jit(solution)/shard_map/all_to_all | solution.py:260
  31.6 21.4 %copy-start.1 = (bf16[1024,256]{1,0:T(8,128)(2,1)S(1)}, bf16[1024,256]{1,0:T(8,128)(2,1)}, u32[]{:S(2)}) copy-start(bf16[1024,256]{1,0:T(8,128)(2,1)} %k_ref.5) | copy-start | bytes 1572868
  31.7 21.4 %copy-start.2 = (bf16[1024,256]{1,0:T(8,128)(2,1)S(1)}, bf16[1024,256]{1,0:T(8,128)(2,1)}, u32[]{:S(2)}) copy-start(bf16[1024,256]{1,0:T(8,128)(2,1)} %v_ref.5) | copy-start | bytes 1572868
  31.7 21.4 %copy-start.3 = (bf16[1024,256]{1,0:T(8,128)(2,1)S(1)}, bf16[1024,256]{1,0:T(8,128)(2,1)}, u32[]{:S(2)}) copy-start(bf16[1024,256]{1,0:T(8,128)(2,1)} %g_ref.5) | copy-start | bytes 1572868
  54.4 3.7 %collective-permute-start = (f32[8,128]{1,0:T(8,128)S(1)}, f32[8,128]{1,0:T(8,128)S(1)}, u32[]{:S(2)}, u32[]{:S(2)}) collective-permute-start(f32[8,128]{1,0:T(8,128)S(1)} %peak.1), channel_id=1, source_target_pairs={{0,1},{1,0},{2,3},{3,2},{4,5},{5,4},{6,7},{7,6},{8,9},{9,8},{10,11... | collective-permute-start | bytes 12296 | tf_op jit(solution)/shard_map/ppermute | solution.py:294
  58.1 4.8 %collective-permute-start.1 = (f32[8,128]{1,0:T(8,128)S(1)}, f32[8,128]{1,0:T(8,128)S(1)}, u32[]{:S(2)}, u32[]{:S(2)}) collective-permute-start(f32[8,128]{1,0:T(8,128)S(1)} %max.6), channel_id=1, source_target_pairs={{0,3},{1,2},{2,1},{3,0},{4,7},{5,6},{6,5},{7,4},{8,11},{9,10},{10,... | collective-permute-start | bytes 12296 | tf_op jit(solution)/shard_map/ppermute | solution.py:294
  62.9 5.2 %collective-permute-start.2 = (f32[8,128]{1,0:T(8,128)S(1)}, f32[8,128]{1,0:T(8,128)S(1)}, u32[]{:S(2)}, u32[]{:S(2)}) collective-permute-start(f32[8,128]{1,0:T(8,128)S(1)} %max.7.peaks_ref), channel_id=1, source_target_pairs={{0,4},{1,5},{2,6},{3,7},{4,0},{5,1},{6,2},{7,3},{8,12},{9,13},{10,... | collective-permute-start | bytes 12296 | tf_op jit(solution)/shard_map/ppermute | solution.py:295
